TPU v7x, 32 devices: a whole 2x2x4 slice. The times are simulated.
32 devices in a mesh: seq: 8 (over z, y), head: 4 (over x, core).
Axes of the slice: x: 2, y: 2, z: 4, core: 2. Of those that a mesh axis runs over, the one named last changes fastest.
Arguments:
- hidden_in: bfloat16 [2048, 1024], P('seq'), may hold values from -6 to 6
- seg_ids: int32 [2048], replicated, may hold values from 0 to 3, never falling along the last dimension, each value on 1 to 1024 neighbouring positions
- norm_gain: float32 [2, 1024], replicated, may hold values from 0.5 to 1.5
- w_z: bfloat16 [2, 1024, 2048], P(None, None, 'head'), may hold values from -0.1875 to 0.1875
- w_x: bfloat16 [2, 1024, 2048], P(None, None, 'head'), may hold values from -0.1875 to 0.1875
- w_bc: bfloat16 [2, 1024, 256], replicated, may hold values from -0.1875 to 0.1875
- w_dt: bfloat16 [2, 1024, 32], P(None, None, 'head'), may hold values from -0.1875 to 0.1875
- conv_x_w: float32 [2, 4, 2048], P(None, None, 'head'), may hold values from -3 to 3
- conv_x_b: float32 [2, 2048], P(None, 'head'), may hold values from -3 to 3
- conv_bc_w: float32 [2, 4, 256], replicated, may hold values from -3 to 3
- conv_bc_b: float32 [2, 256], replicated, may hold values from -3 to 3
- dt_bias: float32 [2, 32], P(None, 'head'), may hold values from -4 to -1
- a_log: float32 [2, 32], P(None, 'head'), may hold values from -8 to 1
- d_skip: float32 [2, 32], P(None, 'head'), may hold values from 0.5 to 1.5
- gate_gain: float32 [2, 2048], P(None, 'head'), may hold values from 0.5 to 1.5
- w_out: bfloat16 [2, 2048, 1024], P(None, 'head'), may hold values from -0.125 to 0.125
- out_cot: float32 [2048, 1024], P('seq'), may hold values from -6 to 6
Outputs:
- hidden_out: bfloat16 [2048, 1024], P('seq')
- grad_in: float32 [2048, 1024], P('seq')
- g_norm_gain: float32 [2, 1024], P(None, 'seq')
- g_w_z: float32 [2, 1024, 2048], P(None, 'seq', 'head')
- g_w_x: float32 [2, 1024, 2048], P(None, 'seq', 'head')
- g_w_bc: float32 [2, 1024, 256], P(None, 'seq')
- g_w_dt: float32 [2, 1024, 32], P(None, 'seq', 'head')
- g_conv_x_w: float32 [2, 4, 2048], P(None, None, 'head')
- g_conv_x_b: float32 [2, 2048], P(None, 'head')
- g_conv_bc_w: float32 [2, 4, 256], replicated
- g_conv_bc_b: float32 [2, 256], replicated
- g_dt_bias: float32 [2, 32], P(None, 'head')
- g_a_log: float32 [2, 32], P(None, 'head')
- g_d_skip: float32 [2, 32], P(None, 'head')
- g_gate_gain: float32 [2, 2048], P(None, 'head')
- g_w_out: float32 [2, 2048, 1024], P(None, 'head', 'seq')
Inputs may be any that keep to these rules, and one draw needn't show every extreme that they name: seg_ids never falls along the tokens; each document holds at most 1024 tokens and one holds exactly 1024.
All inputs are finite; a program needn't handle non-finite values.
Results may differ from a plain program's by a relative error of at most 0.012.
The roundings to bfloat16 on the way count: a program that leaves them out, or rounds other values in their place, can miss the bound.
Values sent between devices are 32-bit elements; how exact they have to be, the bound alone decides.
No kernel may reach another device: no remote copies, remote signals or barrier semaphores. Data moves between devices by JAX's collectives and lax.ppermute only.
A program may use at most 128 MiB of HBM per device.

v0:
```python
import jax
import jax.numpy as jnp
from jax import lax
from jax.sharding import PartitionSpec as P

SPAN = 256


eps = 1e-05
highest = lax.Precision.HIGHEST


def from_behind(value, axis, steps):
    count = lax.axis_size(axis)
    leading, last = (max(0, -steps), min(count, count - steps))
    return lax.ppermute(value, axis, [(source, source + steps) for source in range(leading, last)])


def carried_in_2(part, axis, combine, identity, reverse):
    count = lax.axis_size(axis)
    place = lax.axis_index(axis)
    ahead = count - 1 - place if reverse else place
    gathered = jax.tree.map(lambda a: lax.all_gather(a, axis), part)
    state = jax.tree.map(lambda a, e: jnp.zeros_like(a) + jnp.asarray(e, a.dtype), part, identity)

    def one(step, state):
        source = count - 1 - step if reverse else step
        return combine(
            state, jax.tree.map(lambda a: lax.dynamic_index_in_dim(a, source, 0, False), gathered)
        )

    return lax.fori_loop(0, ahead, one, state)


def contract_rows(left, right):
    return lax.dot_general(
        left, right, (((0,), (0,)), ((), ())), preferred_element_type=jnp.float32
    )


def contract_cols(left, right):
    return lax.dot_general(
        left, right, (((1,), (1,)), ((), ())), preferred_element_type=jnp.float32
    )


def in_norm(resid, gain_row):
    return resid * lax.rsqrt(jnp.mean(resid * resid, axis=1) + eps)[:, None] * gain_row[None, :]


def causal_conv(inputs, edge_rows, weights, biases, seg_ext):
    tok_rows = inputs.shape[0]
    tap_count = weights.shape[0]
    extended = jnp.concatenate([edge_rows, inputs], axis=0)
    own_seg = seg_ext[tap_count - 1 :]
    summed = jnp.zeros_like(inputs) + biases[None, :]
    for offset in range(tap_count):
        keep_mask = (seg_ext[offset : offset + tok_rows] == own_seg).astype(jnp.float32)
        summed = (
            summed
            + weights[offset][None, :] * extended[offset : offset + tok_rows] * keep_mask[:, None]
        )
    return summed


def front_end(x_proj, bc_proj, dt_proj, x_edge, bc_edge, layer_params, seg_ext, head_count):
    conv_xw, conv_xb, conv_bw, conv_bb, dt_shift, log_rate, skip_gain = layer_params
    x_conv = jax.nn.silu(causal_conv(x_proj, x_edge, conv_xw, conv_xb, seg_ext))
    bc_conv = jax.nn.silu(causal_conv(bc_proj, bc_edge, conv_bw, conv_bb, seg_ext))
    state_width = bc_conv.shape[1] // 2
    step_size = jax.nn.softplus(dt_proj + dt_shift[None, :])
    log_decay = -step_size * jnp.exp(log_rate)[None, :]
    x_heads = x_conv.reshape(x_conv.shape[0], head_count, -1)
    return (x_heads, bc_conv[:, :state_width], bc_conv[:, state_width:], step_size, log_decay)


def span_states(x_heads, b_mat, c_mat, step_size, log_decay, own_seg, seg_before, span_len):
    tok_rows, head_count, head_width = x_heads.shape
    state_width = b_mat.shape[1]
    span_count = tok_rows // span_len
    entry_weight = (
        jnp.exp(jnp.cumsum(log_decay, axis=0))
        * (own_seg == seg_before).astype(jnp.float32)[:, None]
    )
    earlier_seg = jnp.concatenate([seg_before[None], own_seg[:-1]])
    span_prev = earlier_seg.reshape(span_count, span_len)[:, 0]
    position = jnp.arange(span_len)
    causal = position[:, None] >= position[None, :]

    def advance(carried, pieces):
        x_part, b_part, c_part, dt_part, decay_part, seg_part, prev_seg = pieces
        cumul = jnp.cumsum(decay_part, axis=0)
        same_doc = (seg_part[:, None] == seg_part[None, :]) & causal
        gaps = cumul[:, None, :] - cumul[None, :, :]
        kernel = jnp.exp(jnp.where(same_doc[:, :, None], gaps, -1e30))
        inner_prod = jnp.dot(c_part, b_part.T, precision=highest)
        scores = inner_prod[:, :, None] * kernel * dt_part[None, :, :]
        y_intra = jnp.einsum("ijh,jhp->ihp", scores, x_part, precision=highest)
        into = jnp.exp(cumul) * (seg_part == prev_seg).astype(jnp.float32)[:, None]
        y_inter = jnp.einsum("is,hps->ihp", c_part, carried, precision=highest) * into[:, :, None]
        to_end = (
            jnp.exp(cumul[-1][None, :] - cumul)
            * (seg_part == seg_part[-1]).astype(jnp.float32)[:, None]
            * dt_part
        )
        updated = carried * into[-1][:, None, None] + jnp.einsum(
            "jh,jhp,js->hps", to_end, x_part, b_part, precision=highest
        )
        return (updated, y_intra + y_inter)

    start_state = jnp.zeros((head_count, head_width, state_width), jnp.float32)
    pieces = (
        x_heads.reshape(span_count, span_len, head_count, head_width),
        b_mat.reshape(span_count, span_len, state_width),
        c_mat.reshape(span_count, span_len, state_width),
        step_size.reshape(span_count, span_len, head_count),
        log_decay.reshape(span_count, span_len, head_count),
        own_seg.reshape(span_count, span_len),
        span_prev,
    )
    final_state, outputs = lax.scan(jax.checkpoint(advance), start_state, pieces)
    return (outputs.reshape(tok_rows, head_count, head_width), final_state, entry_weight)


def mixer_full(
    z_proj, x_proj, bc_proj, dt_proj, x_edge, bc_edge, layer_params, incoming, seg_ext, span_len
):
    head_count = layer_params[4].shape[0]
    tap_count = layer_params[0].shape[0]
    x_heads, b_mat, c_mat, step_size, log_decay = front_end(
        x_proj, bc_proj, dt_proj, x_edge, bc_edge, layer_params, seg_ext, head_count
    )
    own_seg = seg_ext[tap_count - 1 :]
    seg_before = seg_ext[tap_count - 2]
    y_local, local_state, entry_weight = span_states(
        x_heads, b_mat, c_mat, step_size, log_decay, own_seg, seg_before, span_len
    )
    carried_in = (
        jnp.einsum("ts,hps->thp", c_mat, incoming, precision=highest) * entry_weight[:, :, None]
    )
    mixed = y_local + carried_in + layer_params[6][None, :, None] * x_heads
    gated = mixed.reshape(mixed.shape[0], -1) * jax.nn.silu(z_proj)
    final_state = local_state + entry_weight[-1][:, None, None] * incoming
    return ((gated, final_state), (entry_weight, c_mat))


def combine_states(earlier, later):
    return (earlier[0] * later[0], later[0][:, None, None] * earlier[1] + later[1])


def local(
    hidden_in,
    seg_ids,
    norm_gain,
    w_z,
    w_x,
    w_bc,
    w_dt,
    conv_x_w,
    conv_x_b,
    conv_bc_w,
    conv_bc_b,
    dt_bias,
    a_log,
    d_skip,
    gate_gain,
    w_out,
    out_cot,
):
    tok_rows = hidden_in.shape[0]
    layer_count = w_z.shape[0]
    head_count = w_dt.shape[2]
    inner_local = w_z.shape[2]
    head_width = inner_local // head_count
    state_width = w_bc.shape[2] // 2
    inner_total = inner_local * lax.axis_size("head")
    tap_count = conv_x_w.shape[1]
    edge_start = tok_rows - tap_count + 1
    padded = jnp.concatenate([jnp.full((tap_count - 1,), -1, jnp.int32), seg_ids])
    seg_ext = lax.dynamic_slice_in_dim(
        padded, lax.axis_index("seq") * tok_rows, tok_rows + tap_count - 1
    )
    unit_pair = (
        jnp.ones((head_count,), jnp.float32),
        jnp.zeros((head_count, head_width, state_width), jnp.float32),
    )

    def project(normed, layer_idx):
        return (
            jnp.dot(normed, w_z[layer_idx], preferred_element_type=jnp.float32),
            jnp.dot(normed, w_x[layer_idx], preferred_element_type=jnp.float32),
            jnp.dot(normed, w_bc[layer_idx], preferred_element_type=jnp.float32),
            jnp.dot(normed, w_dt[layer_idx], preferred_element_type=jnp.float32),
        )

    def params_of(layer_idx):
        return (
            conv_x_w[layer_idx],
            conv_x_b[layer_idx],
            conv_bc_w[layer_idx],
            conv_bc_b[layer_idx],
            dt_bias[layer_idx],
            a_log[layer_idx],
            d_skip[layer_idx],
        )

    residual = hidden_in.astype(jnp.float32)
    saved = []
    for layer_idx in range(layer_count):
        normed = in_norm(residual, norm_gain[layer_idx]).astype(jnp.bfloat16)
        z_proj, x_proj, bc_proj, dt_proj = project(normed, layer_idx)
        x_edge, bc_edge = from_behind((x_proj[edge_start:], bc_proj[edge_start:]), "seq", 1)
        layer_params = params_of(layer_idx)
        x_heads, b_mat, c_mat, step_size, log_decay = front_end(
            x_proj, bc_proj, dt_proj, x_edge, bc_edge, layer_params, seg_ext, head_count
        )
        y_local, local_state, entry_weight = span_states(
            x_heads,
            b_mat,
            c_mat,
            step_size,
            log_decay,
            seg_ext[tap_count - 1 :],
            seg_ext[tap_count - 2],
            SPAN,
        )
        incoming = carried_in_2(
            (entry_weight[-1], local_state), "seq", combine_states, unit_pair, False
        )[1]
        carried_in = (
            jnp.einsum("ts,hps->thp", c_mat, incoming, precision=highest) * entry_weight[:, :, None]
        )
        mixed = y_local + carried_in + d_skip[layer_idx][None, :, None] * x_heads
        gated = mixed.reshape(tok_rows, inner_local) * jax.nn.silu(z_proj)
        square_sum = lax.psum(jnp.sum(gated * gated, axis=1), "head")
        scale = lax.rsqrt(square_sum / inner_total + eps)
        gated_normed = (gated * scale[:, None] * gate_gain[layer_idx][None, :]).astype(jnp.bfloat16)
        branch = lax.psum(
            jnp.dot(gated_normed, w_out[layer_idx], preferred_element_type=jnp.float32), "head"
        )
        saved.append((residual, x_edge, bc_edge, incoming, scale))
        residual = residual + branch
    hidden_out = residual.astype(jnp.bfloat16)
    cotangent = out_cot
    big_lists = [[None] * layer_count for index in range(6)]
    small_lists = [[None] * layer_count for index in range(8)]
    for layer_idx in reversed(range(layer_count)):
        residual, x_edge, bc_edge, incoming, scale = saved[layer_idx]
        normed_f, norm_pull = jax.vjp(in_norm, residual, norm_gain[layer_idx])
        normed = normed_f.astype(jnp.bfloat16)
        z_proj, x_proj, bc_proj, dt_proj = project(normed, layer_idx)

        def local_mixer(zp_in, xp_in, bp_in, dp_in, xe_in, be_in, lp_in, inc_in):
            return mixer_full(
                zp_in, xp_in, bp_in, dp_in, xe_in, be_in, lp_in, inc_in, seg_ext, SPAN
            )

        outputs, mixer_pull, extras = jax.vjp(
            local_mixer,
            z_proj,
            x_proj,
            bc_proj,
            dt_proj,
            x_edge,
            bc_edge,
            params_of(layer_idx),
            incoming,
            has_aux=True,
        )
        gated = outputs[0]
        entry_weight, c_mat = extras
        gamma = gate_gain[layer_idx][None, :]
        gated_normed = (gated * scale[:, None] * gamma).astype(jnp.bfloat16)
        cot_b = cotangent.astype(jnp.bfloat16)
        big_lists[4][layer_idx] = contract_rows(gated_normed, cot_b)
        d_gated_normed = contract_cols(cot_b, w_out[layer_idx])
        small_lists[7][layer_idx] = jnp.sum(d_gated_normed * gated * scale[:, None], axis=0)
        cross = lax.psum(jnp.sum(gated * gamma * d_gated_normed, axis=1), "head")
        d_gated = (
            scale[:, None] * gamma * d_gated_normed
            - gated * (scale * scale * scale * cross / inner_total)[:, None]
        )
        d_mixed = (d_gated * jax.nn.silu(z_proj)).reshape(tok_rows, head_count, head_width)
        local_pull = jnp.einsum("th,thp,ts->hps", entry_weight, d_mixed, c_mat, precision=highest)
        d_final = carried_in_2(
            (entry_weight[-1], local_pull), "seq", combine_states, unit_pair, True
        )[1]
        d_z, d_x, d_bc, d_dt, d_xe, d_be, d_params, d_incoming = mixer_pull((d_gated, d_final))
        bc_summed, be_summed, grad_cbw, grad_cbb = lax.psum(
            (d_bc, d_be, d_params[2], d_params[3]), "head"
        )
        next_x, next_bc = from_behind((d_xe, be_summed), "seq", -1)
        d_x = d_x + jnp.concatenate(
            [jnp.zeros((edge_start, inner_local), jnp.float32), next_x], axis=0
        )
        d_bc_full = bc_summed + jnp.concatenate(
            [jnp.zeros((edge_start, 2 * state_width), jnp.float32), next_bc], axis=0
        )
        d_z_b = d_z.astype(jnp.bfloat16)
        d_x_b = d_x.astype(jnp.bfloat16)
        d_dt_b = d_dt.astype(jnp.bfloat16)
        d_bc_b = d_bc_full.astype(jnp.bfloat16)
        own_part = (
            contract_cols(d_z_b, w_z[layer_idx])
            + contract_cols(d_x_b, w_x[layer_idx])
            + contract_cols(d_dt_b, w_dt[layer_idx])
        )
        summed_part = lax.psum(own_part, "head")
        d_normed = summed_part + contract_cols(d_bc_b, w_bc[layer_idx])
        d_resid, d_gain = norm_pull(d_normed)
        cotangent = cotangent + d_resid
        big_lists[0][layer_idx] = contract_rows(normed, d_z_b)
        big_lists[1][layer_idx] = contract_rows(normed, d_x_b)
        big_lists[2][layer_idx] = contract_rows(normed, d_bc_b)
        big_lists[3][layer_idx] = contract_rows(normed, d_dt_b)
        big_lists[5][layer_idx] = d_gain
        small_lists[0][layer_idx] = d_params[0]
        small_lists[1][layer_idx] = d_params[1]
        small_lists[2][layer_idx] = grad_cbw
        small_lists[3][layer_idx] = grad_cbb
        small_lists[4][layer_idx] = d_params[4]
        small_lists[5][layer_idx] = d_params[5]
        small_lists[6][layer_idx] = d_params[6]
    grad_wz, grad_wx, grad_wbc, grad_wdt, grad_wout, grad_gain = (
        lax.psum_scatter(jnp.stack(big_lists[0]), "seq", scatter_dimension=1, tiled=True),
        lax.psum_scatter(jnp.stack(big_lists[1]), "seq", scatter_dimension=1, tiled=True),
        lax.psum_scatter(jnp.stack(big_lists[2]), "seq", scatter_dimension=1, tiled=True),
        lax.psum_scatter(jnp.stack(big_lists[3]), "seq", scatter_dimension=1, tiled=True),
        lax.psum_scatter(jnp.stack(big_lists[4]), "seq", scatter_dimension=2, tiled=True),
        lax.psum_scatter(jnp.stack(big_lists[5]), "seq", scatter_dimension=1, tiled=True),
    )
    small_sums = lax.psum(
        (
            jnp.stack(small_lists[0]),
            jnp.stack(small_lists[1]),
            jnp.stack(small_lists[2]),
            jnp.stack(small_lists[3]),
            jnp.stack(small_lists[4]),
            jnp.stack(small_lists[5]),
            jnp.stack(small_lists[6]),
            jnp.stack(small_lists[7]),
        ),
        "seq",
    )
    return (
        hidden_out,
        cotangent,
        grad_gain,
        grad_wz,
        grad_wx,
        grad_wbc,
        grad_wdt,
        small_sums[0],
        small_sums[1],
        small_sums[2],
        small_sums[3],
        small_sums[4],
        small_sums[5],
        small_sums[6],
        small_sums[7],
        grad_wout,
    )


def solution(mesh):
    return jax.shard_map(
        local,
        mesh=mesh,
        in_specs=(
            P("seq", None),
            P(),
            P(),
            P(None, None, "head"),
            P(None, None, "head"),
            P(),
            P(None, None, "head"),
            P(None, None, "head"),
            P(None, "head"),
            P(),
            P(),
            P(None, "head"),
            P(None, "head"),
            P(None, "head"),
            P(None, "head"),
            P(None, "head", None),
            P("seq", None),
        ),
        out_specs=(
            P("seq", None),
            P("seq", None),
            P(None, "seq"),
            P(None, "seq", "head"),
            P(None, "seq", "head"),
            P(None, "seq", None),
            P(None, "seq", "head"),
            P(None, None, "head"),
            P(None, "head"),
            P(),
            P(),
            P(None, "head"),
            P(None, "head"),
            P(None, "head"),
            P(None, "head"),
            P(None, "head", "seq"),
        ),
        check_vma=False,
    )
```

profile of v0, /device:TPU:0, one launch (start us, length us, event | category | flops | bytes accessed | tf_op | source)
XLA Modules:
  0.0 1100.6 jit_solution(9877128838317728424)
XLA Ops:
  33.0 18.2 %all-gather.4 = f32[8,1,8]{2,1,0:T(1,128)S(1)} all-gather(f32[1,1,8]{2,1,0:T(1,128)S(1)} %bitcast.653), channel_id=1, replica_groups=mesh['seq'=8,'head'=4] {'seq'}, dimensions={0}, use_global_device_ids=true | all-gather | bytes 288 | tf_op jit(solution)/shard_map/all_gather | solution.py:23
  53.5 28.8 %all-gather.13.cloned.1.call-done = f32[64,64,128]{2,1,0:T(8,128)} async-done(((f32[8,64,128]{2,1,0:T(8,128)}), f32[64,64,128]{2,1,0:T(8,128)}) %all-gather.13.cloned.1.call-update) | async-done | bytes 2097168 | tf_op jit(solution)/shard_map/all_gather | solution.py:23
  88.4 5.7 psum.168
  97.7 42.1 %all-reduce.55.cloned.1.call-done = f32[256,1024]{1,0:T(8,128)} async-done(((f32[256,1024]{1,0:T(8,128)}), f32[256,1024]{1,0:T(8,128)}) %all-reduce.55.cloned.1.call-update) | async-done | bytes 1048592 | tf_op jit(solution)/shard_map/psum | solution.py:238
  162.1 19.8 %all-gather.5 = f32[8,1,8]{2,1,0:T(1,128)S(1)} all-gather(f32[1,1,8]{2,1,0:T(1,128)S(1)} %bitcast.654), channel_id=1, replica_groups=mesh['seq'=8,'head'=4] {'seq'}, dimensions={0}, use_global_device_ids=true | all-gather | bytes 288 | tf_op jit(solution)/shard_map/all_gather | solution.py:23
  185.7 25.7 %all-gather.15.cloned.1.call-done = f32[64,64,128]{2,1,0:T(8,128)} async-done(((f32[8,64,128]{2,1,0:T(8,128)}), f32[64,64,128]{2,1,0:T(8,128)}) %all-gather.15.cloned.1.call-update) | async-done | bytes 2097168 | tf_op jit(solution)/shard_map/all_gather | solution.py:23
  237.3 6.6 psum.172
  251.3 26.0 %all-gather.6 = f32[8,1,8]{2,1,0:T(1,128)} all-gather(f32[1,1,8]{2,1,0:T(1,128)S(1)} %bitcast.655), channel_id=1, replica_groups=mesh['seq'=8,'head'=4] {'seq'}, dimensions={0}, use_global_device_ids=true | all-gather | bytes 288 | tf_op jit(solution)/shard_map/all_gather | solution.py:23
  283.5 21.6 %all-gather.17.cloned.1.call-done = f32[64,64,128]{2,1,0:T(8,128)} async-done(((f32[8,64,128]{2,1,0:T(8,128)}), f32[64,64,128]{2,1,0:T(8,128)}) %all-gather.17.cloned.1.call-update) | async-done | bytes 2097168 | tf_op jit(solution)/shard_map/all_gather | solution.py:23
  305.1 12.8 %while.34 = (s32[]{:T(128)}, f32[8,64,128]{2,1,0:T(8,128)S(1)}, s32[]{:T(128)}, f32[8,8]{1,0:T(8,128)}, f32[8,8,64,128]{3,2,1,0:T(8,128)}, /*index=5*/s32[]{:T(128)}, s32[]{:T(128)}, s32[]{:T(128)}, s32[]{:T(128)}) while((s32[]{:T(128)}, f32[8,64,128]{2,1,0:T(8,128)S(1)}, s32[]{:T(128)}, f32[8,8]{1,0:T(8,128)}, ...), condition=%wide.region_21.23_spmd, body=%wide.region_20.22_spmd.sunk | while | flops 131078 | bytes 786683 | solution.py:32
  383.7 5.6 psum.175
  395.5 26.1 %all-reduce.59.cloned.1.call-done = (f32[256,1024]{1,0:T(8,128)}, f32[256,256]{1,0:T(8,128)}) async-done(((f32[256,1024]{1,0:T(8,128)}, f32[256,256]{1,0:T(8,128)}), (f32[256,1024]{1,0:T(8,128)}, f32[256,256]{1,0:T(8,128)})) %all-reduce.59.cloned.1.call-update) | async-done | bytes 1310736 | tf_op jit(solution)/shard_map/psum | solution.py:308
  428.0 5.9 psum.176
  442.0 21.2 %all-gather.7 = f32[8,1,8]{2,1,0:T(1,128)} all-gather(f32[1,1,8]{2,1,0:T(1,128)S(1)} %bitcast.656), channel_id=1, replica_groups=mesh['seq'=8,'head'=4] {'seq'}, dimensions={0}, use_global_device_ids=true | all-gather | bytes 288 | tf_op jit(solution)/shard_map/all_gather | solution.py:23
  470.2 19.4 %all-gather.19.cloned.1.call-done = f32[64,64,128]{2,1,0:T(8,128)} async-done(((f32[8,64,128]{2,1,0:T(8,128)}), f32[64,64,128]{2,1,0:T(8,128)}) %all-gather.19.cloned.1.call-update) | async-done | bytes 2097168 | tf_op jit(solution)/shard_map/all_gather | solution.py:23
  489.7 12.3 %while.35 = (s32[]{:T(128)}, f32[8,64,128]{2,1,0:T(8,128)S(1)}, s32[]{:T(128)}, f32[8,8]{1,0:T(8,128)}, f32[8,8,64,128]{3,2,1,0:T(8,128)}, /*index=5*/s32[]{:T(128)}, s32[]{:T(128)}, s32[]{:T(128)}, s32[]{:T(128)}) while((s32[]{:T(128)}, f32[8,64,128]{2,1,0:T(8,128)S(1)}, s32[]{:T(128)}, f32[8,8]{1,0:T(8,128)}, ...), condition=%wide.region_46.48_spmd, body=%wide.region_45.47_spmd.sunk | while | flops 131078 | bytes 786683 | solution.py:32
  570.5 12.3 %all-reduce.48 = (f32[3,256]{1,0:T(4,128)S(1)}, f32[1,4,256]{2,1,0:T(4,128)S(1)}, f32[1,4,256]{2,1,0:T(4,128)S(1)}, f32[1,256]{1,0:T(1,128)S(1)}, f32[1,256]{1,0:T(1,128)}) all-reduce(f32[3,256]{1,0:T(4,128)S(1)} %pad_add_fusion.6, f32[1,4,256]{2,1,0:T(4,128)S(1)} %get-tuple-element.799, ...), channel_id=1, replica_groups=mesh['seq'=8,'head'=4] {'head'}, use_global_device_ids=true, to_apply=%region_64.66 | all-reduce | flops 3328 | bytes 26624 | tf_op jit(solution)/shard_map/psum | solution.py:289
  589.1 32.4 %all-reduce.57.cloned.1.call-done = (f32[256,1024]{1,0:T(8,128)}, f32[256,1024]{1,0:T(8,128)}, f32[256,256]{1,0:T(8,128)}) async-done(((f32[256,1024]{1,0:T(8,128)}, f32[256,1024]{1,0:T(8,128)}, f32[256,256]{1,0:T(8,128)}), (f32[256,1024]{1,0:T(8,128)}, f32[256,1024]{1,0:T(8,128)}, f32[256,256]{1,0:T(8,128)})) %all-reduce.57.cloned.1.call-update) | async-done | bytes 2359312 | tf_op jit(solution)/shard_map/psum | solution.py:238
  647.8 38.2 %all-reduce.47 = (f32[2,4,512]{2,1,0:T(4,128)}, f32[2,512]{1,0:T(2,128)}, f32[2,4,256]{2,1,0:T(4,128)}, f32[2,256]{1,0:T(2,128)}, f32[2,8]{1,0:T(2,128)}, /*inde...) all-reduce(f32[2,4,512]{2,1,0:T(4,128)S(1)} %pad_maximum_fusion.9, ...), channel_id=1, replica_groups=mesh['seq'=8,'head'=4] {'seq'}, use_global_device_ids=true, to_apply=%region_81.83 | all-reduce | flops 8752 | bytes 70016 | tf_op jit(solution)/shard_map/psum | solution.py:332
  690.9 54.8 %reduce-scatter.15.cloned.1.call-done = f32[2,128,8]{1,2,0:T(8,128)} async-done(((f32[2,1024,8]{1,2,0:T(8,128)}), f32[2,128,8]{1,2,0:T(8,128)}) %reduce-scatter.15.cloned.1.call-update) | async-done | bytes 8208 | tf_op jit(solution)/shard_map/reduce_scatter | solution.py:328
  745.7 91.4 %reduce-scatter.9.cloned.1.call-done = f32[2,128,512]{2,1,0:T(8,128)} async-done(((f32[2,1024,512]{2,1,0:T(8,128)}), f32[2,128,512]{2,1,0:T(8,128)}) %reduce-scatter.9.cloned.1.call-update) | async-done | bytes 524304 | tf_op jit(solution)/shard_map/reduce_scatter | solution.py:325
  837.1 92.6 %reduce-scatter.17.cloned.1.call-done = f32[2,512,128]{2,1,0:T(8,128)} async-done(((f32[2,512,1024]{2,1,0:T(8,128)}), f32[2,512,128]{2,1,0:T(8,128)}) %reduce-scatter.17.cloned.1.call-update) | async-done | bytes 524304 | tf_op jit(solution)/shard_map/reduce_scatter | solution.py:329
  929.7 72.2 %reduce-scatter.13.cloned.1.call-done = f32[2,128,256]{2,1,0:T(8,128)} async-done(((f32[2,1024,256]{2,1,0:T(8,128)}), f32[2,128,256]{2,1,0:T(8,128)}) %reduce-scatter.13.cloned.1.call-update) | async-done | bytes 262160 | tf_op jit(solution)/shard_map/reduce_scatter | solution.py:327
  1002.0 91.6 %reduce-scatter.11.cloned.1.call-done = f32[2,128,512]{2,1,0:T(8,128)} async-done(((f32[2,1024,512]{2,1,0:T(8,128)}), f32[2,128,512]{2,1,0:T(8,128)}) %reduce-scatter.11.cloned.1.call-update) | async-done | bytes 524304 | tf_op jit(solution)/shard_map/reduce_scatter | solution.py:326
  (788 shorter events, 324.3 us)
Async XLA Ops:
  7.2 75.1 %all-gather.13.cloned.1.call-start = ((), (), s32[]{:S(2)}) async-start(), calls=%async_computation.12 | async-start | bytes 2359296 | tf_op jit(solution)/shard_map/all_gather | solution.py:23
  8.1 133.4 %copy-start.106 = (f32[1,1024]{1,0:T(1,128)}, f32[1,1024]{1,0:T(1,128)S(1)}, u32[]{:S(2)}) copy-start(f32[1,1024]{1,0:T(1,128)S(1)} %get-tuple-element.754) | copy-start | bytes 12292
  11.4 18.5 %collective-permute-start = (f32[3,512]{1,0:T(4,128)S(1)}, f32[3,512]{1,0:T(4,128)S(1)}, u32[]{:S(2)}, u32[]{:S(2)}) collective-permute-start(f32[3,512]{1,0:T(4,128)S(1)} %slice.588), channel_id=1, source_target_pairs={{0,4},{4,8},{8,12},{12,16},{16,20},{20,24},{24,28},{1,5},{5,9},{9,... | collective-permute-start | bytes 18440 | tf_op jit(solution)/shard_map/ppermute | solution.py:16
  16.8 12.1 %collective-permute-start.1 = (f32[3,256]{1,0:T(4,128)S(1)}, f32[3,256]{1,0:T(4,128)S(1)}, u32[]{:S(2)}, u32[]{:S(2)}) collective-permute-start(f32[3,256]{1,0:T(4,128)S(1)} %slice.593), channel_id=1, source_target_pairs={{0,4},{4,8},{8,12},{12,16},{16,20},{20,24},{24,28},{1,5},{5,9},{9,... | collective-permute-start | bytes 9224 | tf_op jit(solution)/shard_map/ppermute | solution.py:16
  32.7 107.1 %all-reduce.55.cloned.1.call-start = ((), (), s32[]{:S(2)}) async-start(), calls=%async_computation.6 | async-start | bytes 2097152 | tf_op jit(solution)/shard_map/psum | solution.py:238
  52.4 175.2 %copy-start.102 = (pred[256,256]{1,0:T(8,128)(4,1)}, pred[256,256]{1,0:T(8,128)(4,1)S(1)}, u32[]{:S(2)}) copy-start(pred[256,256]{1,0:T(8,128)(4,1)S(1)} %compare_and_fusion.2) | copy-start | bytes 196612
  96.9 114.5 %all-gather.15.cloned.1.call-start = ((), (), s32[]{:S(2)}) async-start(), calls=%async_computation.13 | async-start | bytes 2359296 | tf_op jit(solution)/shard_map/all_gather | solution.py:23
  143.7 11.8 %collective-permute-start.2 = (f32[3,512]{1,0:T(4,128)}, f32[3,512]{1,0:T(4,128)S(1)}, u32[]{:S(2)}, u32[]{:S(2)}) collective-permute-start(f32[3,512]{1,0:T(4,128)} %slice.605), channel_id=1, source_target_pairs={{0,4},{4,8},{8,12},{12,16},{16,20},{20,24},{24,28},{1,5},{5,9},{9,... | collective-permute-start | bytes 18440 | tf_op jit(solution)/shard_map/ppermute | solution.py:16
  149.1 4.7 collective-permute-start.3
  153.1 74.5 %copy-start.87 = (f32[256,8]{0,1:T(8,128)}, f32[256,8]{0,1:T(8,128)S(1)}, u32[]{:S(2)}) copy-start(f32[256,8]{0,1:T(8,128)S(1)} %get-tuple-element.552) | copy-start | bytes 24580
  160.8 144.2 %all-gather.17.cloned.1.call-start = ((), (), s32[]{:S(2)}) async-start(), calls=%async_computation.14 | async-start | bytes 2359296 | tf_op jit(solution)/shard_map/all_gather | solution.py:23
  249.7 171.9 %all-reduce.59.cloned.1.call-start = ((), (), s32[]{:S(2)}) async-start(), calls=%async_computation.18 | async-start | bytes 2621440 | tf_op jit(solution)/shard_map/psum | solution.py:308
  360.6 19.7 %collective-permute-start.4 = (f32[3,512]{1,0:T(4,128)}, f32[3,512]{1,0:T(4,128)}, u32[]{:S(2)}, u32[]{:S(2)}) collective-permute-start(f32[3,512]{1,0:T(4,128)} %pad_add_fusion.5), channel_id=1, source_target_pairs={{4,0},{8,4},{12,8},{16,12},{20,16},{24,20},{28,24},{5,1},{9,5},{13... | collective-permute-start | bytes 18440 | tf_op jit(solution)/shard_map/ppermute | solution.py:16
  383.0 106.7 %all-gather.19.cloned.1.call-start = ((), (), s32[]{:S(2)}) async-start(), calls=%async_computation.15 | async-start | bytes 2359296 | tf_op jit(solution)/shard_map/all_gather | solution.py:23
  389.4 6.1 collective-permute-start.5
  439.7 181.7 %all-reduce.57.cloned.1.call-start = ((), (), s32[]{:S(2)}) async-start(), calls=%async_computation.17 | async-start | bytes 4718592 | tf_op jit(solution)/shard_map/psum | solution.py:238
  544.8 18.9 %collective-permute-start.6 = (f32[3,512]{1,0:T(4,128)}, f32[3,512]{1,0:T(4,128)}, u32[]{:S(2)}, u32[]{:S(2)}) collective-permute-start(f32[3,512]{1,0:T(4,128)} %pad_add_fusion.4), channel_id=1, source_target_pairs={{4,0},{8,4},{12,8},{16,12},{20,16},{24,20},{28,24},{5,1},{9,5},{13... | collective-permute-start | bytes 18440 | tf_op jit(solution)/shard_map/ppermute | solution.py:16
  566.3 123.1 %reduce-scatter.19.cloned.1.call-start = ((), (), s32[]{:S(2)}) async-start(), calls=%async_computation.16 | async-start | bytes 589824
  582.8 6.2 collective-permute-start.7
  625.3 120.4 %reduce-scatter.15.cloned.1.call-start = ((), (), s32[]{:S(2)}) async-start(), calls=%async_computation.10 | async-start | bytes 73728 | tf_op jit(solution)/shard_map/reduce_scatter | solution.py:328
  626.0 211.1 %reduce-scatter.9.cloned.1.call-start = ((), (), s32[]{:S(2)}) async-start(), calls=%async_computation.7 | async-start | bytes 4718592 | tf_op jit(solution)/shard_map/reduce_scatter | solution.py:325
  630.7 299.0 %reduce-scatter.17.cloned.1.call-start = ((), (), s32[]{:S(2)}) async-start(), calls=%async_computation.11 | async-start | bytes 4718592 | tf_op jit(solution)/shard_map/reduce_scatter | solution.py:329
  636.6 365.3 %reduce-scatter.13.cloned.1.call-start = ((), (), s32[]{:S(2)}) async-start(), calls=%async_computation.9 | async-start | bytes 2359296 | tf_op jit(solution)/shard_map/reduce_scatter | solution.py:327
  640.8 452.8 %reduce-scatter.11.cloned.1.call-start = ((), (), s32[]{:S(2)}) async-start(), calls=%async_computation.8 | async-start | bytes 4718592 | tf_op jit(solution)/shard_map/reduce_scatter | solution.py:326
  (229 other events, 2019.1 us)
Sparse Core Ops, SparseCore 0:
  32.9 49.3 all-gather.12
  97.0 42.7 all-reduce.54
  161.0 50.4 all-gather.14
  249.8 55.2 all-gather.16
  383.1 38.4 all-reduce.58
  439.9 49.7 all-gather.18
  566.4 54.9 all-reduce.56
  625.4 62.7 reduce-scatter.18
  691.9 53.7 reduce-scatter.14
  749.8 87.3 reduce-scatter.8
  841.3 88.3 reduce-scatter.16
  933.7 68.2 reduce-scatter.12
  1006.2 87.3 reduce-scatter.10
where the time goes:
time: 1110 us; the launch traced here: 1100 us
  waiting for transfers between devices  604 us (54%)
  blocking collectives  165 us (15%)
  matrix products  117 us (11%)
  other arithmetic  112 us (10%)
  local copies, waits for them, and re-layouts  62 us (6%)
  starting transfers between devices  21.9 us (2%)
  between operations  17.3 us (2%)
    all_gather x4, waiting for transfers between devices, carried_in_2(): gathered = jax.tree.map(lambda a: lax.all_gather(a, axis), part)  95.5 us
    reduce_scatter x1, waiting for transfers between devices, local(): lax.psum_scatter(jnp.stack(big_lists[4]), 'seq', scatter_dimension=2, til...  92.6 us
    reduce_scatter x1, waiting for transfers between devices, local(): lax.psum_scatter(jnp.stack(big_lists[1]), 'seq', scatter_dimension=1, til...  91.6 us
    reduce_scatter x1, waiting for transfers between devices, local(): lax.psum_scatter(jnp.stack(big_lists[0]), 'seq', scatter_dimension=1, til...  91.4 us
    all_gather x4, blocking collectives, carried_in_2(): gathered = jax.tree.map(lambda a: lax.all_gather(a, axis), part)  85.3 us
    psum x2, waiting for transfers between devices, local(): lax.psum(jnp.dot(gated_normed, w_out[layer_idx], preferred_element_type=j...  74.5 us
    reduce_scatter x1, waiting for transfers between devices, local(): lax.psum_scatter(jnp.stack(big_lists[2]), 'seq', scatter_dimension=1, til...  72.2 us
    reduce_scatter x1, waiting for transfers between devices, local(): lax.psum_scatter(jnp.stack(big_lists[3]), 'seq', scatter_dimension=1, til...  54.8 us
  transfers between devices with their start and end apart: 21, of which 14 were waited for; matrix products, arithmetic and copies ran while one was open for 10% of the time, Pallas kernels for 0%

commit v1 on v0

v1 whole, which is shorter than its diff:
```python
import functools

import jax
import jax.numpy as jnp
from jax import lax
from jax.experimental import pallas as pl
from jax.experimental.pallas import tpu as pltpu
from jax.sharding import PartitionSpec as P

eps = 1e-05
F32, BF = jnp.float32, jnp.bfloat16
NN, NT, TN = ((1,), (0,)), ((1,), (1,)), ((0,), (0,))
HALO = 8


def swap(value, axis, mask):
    count = lax.axis_size(axis)
    return lax.ppermute(value, axis, [(i, i ^ mask) for i in range(count)])


def rotate(value, axis, steps):
    count = lax.axis_size(axis)
    return lax.ppermute(value, axis, [(i, (i + steps) % count) for i in range(count)])


def bit_of(axis, bit):
    return (lax.axis_index(axis) >> bit) & 1


def bits_of(axis):
    return lax.axis_size(axis).bit_length() - 1


def halves(value, which, dim):
    half = value.shape[dim] // 2
    keep = lax.dynamic_slice_in_dim(value, which * half, half, dim)
    send = lax.dynamic_slice_in_dim(value, (1 - which) * half, half, dim)
    return keep, send


def scatter_sum(value, axis, dim):
    for bit in range(bits_of(axis)):
        keep, send = halves(value, bit_of(axis, bit), dim)
        value = keep + swap(send, axis, 1 << bit)
    return value


def gather_back(value, axis, dim):
    for bit in reversed(range(bits_of(axis))):
        other = swap(value, axis, 1 << bit)
        first = bit_of(axis, bit) == 0
        value = jnp.where(
            first,
            jnp.concatenate([value, other], dim),
            jnp.concatenate([other, value], dim),
        )
    return value


def own_piece(value, axis, dim):
    for bit in range(bits_of(axis)):
        half = value.shape[dim] // 2
        value = lax.dynamic_slice_in_dim(value, bit_of(axis, bit) * half, half, dim)
    return value


def mask_of(bit):
    return 1 << bit if bit < 2 else 3 << (bit - 1)


def seq_scatter(value, order):
    count = bits_of("seq")
    rows, cols = value.shape
    value = value.reshape((2,) * count + (rows >> count, cols))
    top = list(reversed(range(count)))
    for bit in order:
        dim = top.index(bit)
        keep, send = halves(value, bit_of("seq", bit), dim)
        value = keep + swap(send, "seq", mask_of(bit))
    return value.reshape(rows >> count, cols)


def seq_sum(value):
    for bit in range(bits_of("seq")):
        value = value + swap(value, "seq", mask_of(bit))
    return value


def head_sum(value):
    for bit in range(bits_of("head")):
        value = value + swap(value, "head", 1 << bit)
    return value


def carried(message, heads, reverse):
    cols = message.shape[1]
    rows = message.shape[0] - heads
    state = message[:rows].reshape(heads, rows // heads, cols)
    decay = message[rows:].reshape(heads, 1, cols)
    ahead_s, ahead_d = jnp.zeros_like(state), jnp.ones_like(decay)
    count = bits_of("seq")
    for bit in range(count):
        packed = jnp.concatenate([state.reshape(rows, cols), decay.reshape(heads, cols)], 0)
        got = swap(packed, "seq", mask_of(bit))
        got_s = got[:rows].reshape(heads, rows // heads, cols)
        got_d = got[rows:].reshape(heads, 1, cols)
        upper = bit_of("seq", bit) == 1
        later = jnp.logical_not(upper) if reverse else upper
        ahead_s, ahead_d = (
            jnp.where(later, ahead_d * got_s + ahead_s, ahead_s),
            jnp.where(later, ahead_d * got_d, ahead_d),
        )
        if bit + 1 < count:
            state = jnp.where(later, decay * got_s + state, got_d * state + got_s)
            decay = decay * got_d
    return ahead_s.reshape(rows, cols)


def mm(left, right, dims):
    return lax.dot_general(left, right, (dims, ((), ())), preferred_element_type=F32)


def split2(value):
    high = value.astype(BF)
    return high, (value - high.astype(F32)).astype(BF)


def mm3(left, right, dims):
    lh, ll = split2(left)
    rh, rl = split2(right)
    return mm(lh, rh, dims) + (mm(lh, rl, dims) + mm(ll, rh, dims))


def split3(value):
    high = value.astype(BF)
    rest = value - high.astype(F32)
    mid = rest.astype(BF)
    return high, mid, (rest - mid.astype(F32)).astype(BF)


def sel_right(value, sel, dims):
    return sum(mm(part, sel, dims) for part in split3(value))


def sel_left(sel, value, dims):
    return sum(mm(sel, part, dims) for part in split3(value))


def head_map(heads, inner):
    chan = lax.broadcasted_iota(jnp.int32, (inner, heads), 0)
    head = lax.broadcasted_iota(jnp.int32, (inner, heads), 1)
    return jnp.where(chan // (inner // heads) == head, 1.0, 0.0).astype(BF)


def expand(value, emap):
    return sel_right(value, emap, NT)


def per_head(value, emap):
    return sel_right(value, emap, NN)


def lower(rows):
    row = lax.broadcasted_iota(jnp.int32, (rows, rows), 0)
    col = lax.broadcasted_iota(jnp.int32, (rows, rows), 1)
    return row >= col


def to_column(row_value):
    rows = row_value.shape[1]
    row = lax.broadcasted_iota(jnp.int32, (rows, rows), 0)
    col = lax.broadcasted_iota(jnp.int32, (rows, rows), 1)
    return jnp.sum(jnp.where(row == col, row_value, 0.0), axis=1, keepdims=True)


def row_sums(value):
    ones = jnp.ones((8, value.shape[1]), BF)
    return sel_left(ones, value, NT)[0:1, :]


def sigmoid(value):
    return 1.0 / (1.0 + jnp.exp(-value))


def silu(value):
    return value * sigmoid(value)


def silu_slope(value):
    sig = sigmoid(value)
    return sig * (1.0 + value * (1.0 - sig))


def run(body, outs, *args, blocks=None, scratch=(), flops=2_000_000_000, name=None):
    blocks = blocks or {}

    def whole(shape):
        return pl.BlockSpec(shape, lambda i: (0,) * len(shape))

    in_specs = []
    for place, arg in enumerate(args):
        if place in blocks:
            layer = blocks[place]
            in_specs.append(
                pl.BlockSpec(
                    (pl.Squeezed(),) + arg.shape[1:],
                    functools.partial(lambda l, n, i: (l,) + (0,) * n, layer, arg.ndim - 1),
                )
            )
        else:
            in_specs.append(whole(arg.shape))
    moved = sum(a.size * a.dtype.itemsize for a in args)
    return pl.pallas_call(
        body,
        grid=(1,),
        in_specs=in_specs,
        out_specs=[whole(shape) for shape, kind in outs],
        out_shape=[jax.ShapeDtypeStruct(shape, kind) for shape, kind in outs],
        scratch_shapes=list(scratch),
        cost_estimate=pl.CostEstimate(flops=flops, bytes_accessed=moved, transcendentals=0),
        name=name,
    )(*args)


def k_proj(xn, wz, wx, wbc, wdt, z, x, bc, dt, nb):
    rounded = xn[...].astype(BF)
    nb[...] = rounded
    x[...] = mm(rounded, wx[...], NN)
    bc[...] = mm(rounded, wbc[...], NN)
    dt[...] = mm(rounded, wdt[...], NN)
    z[...] = mm(rounded, wz[...], NN)


def conv_rows(ext, halo_rows, rows, weights, bias, aux):
    total = jnp.broadcast_to(bias, (rows, weights.shape[1]))
    taps = weights.shape[0]
    for tap in range(taps):
        part = ext[pl.ds(halo_rows - taps + 1 + tap, rows), :] * weights[tap : tap + 1, :]
        total = total + (part * aux[:, tap : tap + 1] if tap < taps - 1 else part)
    return total


def k_front(layer, x, bc, dt, edge, aux, cxw, cxb, cbw, cbb, dtb, alog,
            ux, ubc, dts, cum, cumt, msg, ext_x, ext_b):
    rows, inner = x.shape
    heads = dt.shape[1]
    width = bc.shape[1] // 2
    ext_x[0:HALO, :] = edge[:, :inner]
    ext_x[HALO:, :] = x[...]
    ext_b[0:HALO, :] = edge[:, inner:]
    ext_b[HALO:, :] = bc[...]
    masks = aux[...]
    conv_x = conv_rows(ext_x, HALO, rows, cxw[...], cxb[layer : layer + 1, :], masks)
    conv_b = conv_rows(ext_b, HALO, rows, cbw[...], cbb[layer : layer + 1, :], masks)
    ux[...] = conv_x
    ubc[...] = conv_b
    b_mat = silu(conv_b[:, :width])
    raw = dt[...] + dtb[layer : layer + 1, :]
    step = jnp.maximum(raw, 0.0) + jnp.log1p(jnp.exp(-jnp.abs(raw)))
    dts[...] = step
    decay = -step * jnp.exp(alog[layer : layer + 1, :])
    tri = jnp.where(lower(rows), 1.0, 0.0).astype(BF)
    total = sel_left(tri, decay, NN)
    total_t = sum(mm(part, tri, ((0,), (1,))) for part in split3(decay))
    cum[...] = total
    cumt[...] = total_t
    emap = head_map(heads, inner)
    to_end = jnp.exp(total[rows - 1 : rows, :] - total) * masks[:, 3:4] * step
    msg[0:inner, :] = mm3(silu(conv_x) * expand(to_end, emap), b_mat, TN)
    msg[inner:, :] = jnp.broadcast_to(
        jnp.exp(total_t[:, rows - 1 : rows]) * masks[rows - 1 : rows, 4:5], (heads, width)
    )


def head_kernel(cum, cumt, allowed, head):
    gap = cum[:, head : head + 1] - cumt[head : head + 1, :]
    return jnp.exp(jnp.where(allowed, gap, -1e30))


def k_intra(layer, ux, ubc, dts, cum, cumt, segc, segr, dskip, yp):
    rows, inner = ux.shape
    heads = dts.shape[1]
    width = ubc.shape[1] // 2
    per = inner // heads
    emap = head_map(heads, inner)
    x_conv = silu(ux[...])
    bc = silu(ubc[...])
    gram = mm3(bc[:, width:], bc[:, :width], NT)
    allowed = jnp.logical_and(segc[...] == segr[...], lower(rows))
    scaled = x_conv * expand(dts[...], emap)
    skip = x_conv * expand(jnp.broadcast_to(dskip[layer : layer + 1, :], (8, heads)), emap)[0:1, :]
    total, total_t = cum[...], cumt[...]
    group = max(1, 128 // per)
    for first in range(0, heads, group):
        cols = slice(first * per, (first + group) * per)
        sh, sl = split2(scaled[:, cols])
        lane = lax.broadcasted_iota(jnp.int32, (rows, group * per), 1)
        result = skip[:, cols]
        for head in range(first, first + group):
            gh, gl = split2(gram * head_kernel(total, total_t, allowed, head))
            part = mm(gh, sh, NN) + (mm(gh, sl, NN) + mm(gl, sh, NN))
            result = result + jnp.where(lane // per == head - first, part, 0.0)
        yp[:, cols] = result


def k_gate(yp, ubc, cum, aux, z, inc, mixed, gated, ss):
    inner = yp.shape[1]
    heads = cum.shape[1]
    width = ubc.shape[1] // 2
    emap = head_map(heads, inner)
    c_mat = silu(ubc[:, width:])
    into = jnp.exp(cum[...]) * aux[:, 4:5]
    mix = yp[...] + mm3(c_mat, inc[...], NT) * expand(into, emap)
    mixed[...] = mix
    gate = mix * silu(z[...])
    gated[...] = gate
    ss[...] = row_sums(gate * gate)


def k_out(layer, total, gated, ss, gain, wout, gn, part):
    scale = to_column(lax.rsqrt(ss[...] * (1.0 / total) + eps))
    normed = (gated[...] * scale * gain[layer : layer + 1, :]).astype(BF)
    gn[...] = normed
    part[...] = mm(normed, wout[...], NN)


def k_b1(layer, total, cot, wout, gated, ss, gain, cb, dgn, cross, ggain):
    rounded = cot[...].astype(BF)
    cb[...] = rounded
    grad = mm(rounded, wout[...], NT)
    dgn[...] = grad
    scale = to_column(lax.rsqrt(ss[...] * (1.0 / total) + eps))
    both = grad * gated[...]
    cross[...] = row_sums(both * gain[layer : layer + 1, :])
    ggain[...] = jnp.sum(both * scale, axis=0, keepdims=True)


def k_b2(layer, total, dgn, gated, mixed, z, ss, cross, gain, ubc, cum, cumt, aux, dm, dz, msg):
    rows, inner = dgn.shape
    heads = cum.shape[1]
    width = ubc.shape[1] // 2
    emap = head_map(heads, inner)
    scale_row = lax.rsqrt(ss[...] * (1.0 / total) + eps)
    scale = to_column(scale_row)
    pull = to_column(scale_row * scale_row * scale_row * cross[...] * (1.0 / total))
    d_gated = scale * gain[layer : layer + 1, :] * dgn[...] - gated[...] * pull
    zv = z[...]
    grad = d_gated * silu(zv)
    dm[...] = grad
    dz[...] = (d_gated * mixed[...] * silu_slope(zv)).astype(BF)
    masks = aux[...]
    into = jnp.exp(cum[...]) * masks[:, 4:5]
    msg[0:inner, :] = mm3(grad * expand(into, emap), silu(ubc[:, width:]), TN)
    msg[inner:, :] = jnp.broadcast_to(
        jnp.exp(cumt[:, rows - 1 : rows]) * masks[rows - 1 : rows, 4:5], (heads, width)
    )


def k_b3(layer, dm, ux, ubc, dts, cum, cumt, segc, segr, mixed, inc, aux, dskip,
         dx, dbc, dcum, ddt, gskip):
    rows, inner = ux.shape
    heads = dts.shape[1]
    width = ubc.shape[1] // 2
    per = inner // heads
    emap = head_map(heads, inner)
    x_conv = silu(ux[...])
    bc = silu(ubc[...])
    b_mat, c_mat = bc[:, :width], bc[:, width:]
    gram = mm3(c_mat, b_mat, NT)
    allowed = jnp.logical_and(segc[...] == segr[...], lower(rows))
    step = dts[...]
    step_e = expand(step, emap)
    scaled = x_conv * step_e
    grad = dm[...]
    total, total_t = cum[...], cumt[...]
    skip_row = dskip[layer : layer + 1, :]
    skip_e = expand(jnp.broadcast_to(skip_row, (8, heads)), emap)[0:1, :]
    d_gram = jnp.zeros((rows, rows), F32)
    group = max(1, 128 // per)
    plain = []
    for first in range(0, heads, group):
        cols = slice(first * per, (first + group) * per)
        sh, sl = split2(scaled[:, cols])
        lane = lax.broadcasted_iota(jnp.int32, (rows, group * per), 1)
        g_cols = grad[:, cols]
        ch, cl = split2(g_cols)
        result = jnp.zeros((rows, group * per), F32)
        for head in range(first, first + group):
            mine = lane // per == head - first
            fall = head_kernel(total, total_t, allowed, head)
            gh, gl = split2(gram * fall)
            part = mm(gh, ch, TN) + (mm(gh, cl, TN) + mm(gl, ch, TN))
            result = result + jnp.where(mine, part, 0.0)
            mh = jnp.where(mine, ch, jnp.zeros_like(ch))
            ml = jnp.where(mine, cl, jnp.zeros_like(cl))
            outer = mm(mh, sh, NT) + (mm(mh, sl, NT) + mm(ml, sh, NT))
            d_gram = d_gram + outer * fall
        plain.append(result)
    plain = jnp.concatenate(plain, axis=1)
    dx[...] = plain * step_e + grad * skip_e
    into = jnp.exp(total) * aux[:, 4:5]
    dbc[:, :width] = mm3(d_gram, c_mat, TN)
    dbc[:, width:] = mm3(d_gram, b_mat, NN) + mm3(grad * expand(into, emap), inc[...], NN)
    by_col = per_head(x_conv * plain, emap)
    skip_dot = per_head(grad * x_conv, emap)
    ddt[...] = by_col
    dcum[...] = per_head(grad * mixed[...], emap) - skip_row * skip_dot - step * by_col
    gskip[...] = jnp.sum(skip_dot, axis=0, keepdims=True)


def k_b4(layer, ux, ubc, dts, dtp, cum, aux, dx, dbc, dcum, ddt, df, inc, dtb, alog,
         du, dbo, dd, gdtb, galog):
    rows, inner = ux.shape
    heads = dts.shape[1]
    width = ubc.shape[1] // 2
    emap = head_map(heads, inner)
    conv = ux[...]
    x_conv = silu(conv)
    b_mat = silu(ubc[:, :width])
    total, step, masks = cum[...], dts[...], aux[...]
    fin = df[...]
    spread = mm3(b_mat, fin, NT)
    bare = jnp.exp(total[rows - 1 : rows, :] - total) * masks[:, 3:4]
    to_end = bare * step
    to_end_e = expand(to_end, emap)
    dot = per_head(x_conv * spread, emap)
    du[...] = (dx[...] + to_end_e * spread) * silu_slope(conv)
    dbo[:, :width] = dbc[:, :width] + mm3(x_conv * to_end_e, fin, NN)
    dbo[:, width:] = dbc[:, width:]
    used = to_end * dot
    d_cum = dcum[...] - used
    through = per_head(row_sums(fin * inc[...]) + jnp.zeros((8, inner), F32), emap)[0:1, :]
    last = jnp.sum(used, axis=0, keepdims=True) + through * (
        jnp.exp(total[rows - 1 : rows, :]) * masks[rows - 1 : rows, 4:5]
    )
    tri = jnp.where(lower(rows), 1.0, 0.0).astype(BF)
    d_decay = sel_left(tri, d_cum, TN) + last
    rate = jnp.exp(alog[layer : layer + 1, :])
    galog[...] = jnp.sum(-step * rate * d_decay, axis=0, keepdims=True)
    d_raw = (ddt[...] + bare * dot - rate * d_decay) * sigmoid(dtp[...] + dtb[layer : layer + 1, :])
    gdtb[...] = jnp.sum(d_raw, axis=0, keepdims=True)
    dd[...] = d_raw.astype(BF)


def k_conv_back(du, halo, proj, edge, aux, weights, grad, gw, gb, ext_d, ext_p):
    rows = du.shape[0]
    taps = weights.shape[0]
    ext_d[0:rows, :] = du[...]
    ext_d[rows:, :] = halo[...]
    ext_p[0:HALO, :] = edge[...]
    ext_p[HALO:, :] = proj[...]
    masks = aux[...]
    value = du[...]
    total = jnp.zeros_like(value)
    for tap in range(taps):
        back = ext_d[pl.ds(taps - 1 - tap, rows), :] * weights[tap : tap + 1, :]
        seen = ext_p[pl.ds(HALO - taps + 1 + tap, rows), :] * value
        if tap < taps - 1:
            back = back * masks[:, 5 + tap : 6 + tap]
            seen = seen * masks[:, tap : tap + 1]
        total = total + back
        gw[tap : tap + 1, :] = jnp.sum(seen, axis=0, keepdims=True)
    gb[...] = jnp.sum(value, axis=0, keepdims=True)
    grad[...] = total.astype(BF)


def k_dnorm(dz, dxb, dd, dbq, wz, wx, wdt, wbq, own):
    own[...] = (
        mm(dz[...], wz[...], NT)
        + mm(dxb[...], wx[...], NT)
        + mm(dd[...], wdt[...], NT)
        + mm(dbq[...], wbq[...], NT)
    )


def k_round(value, out):
    out[...] = value[...].astype(BF)


def in_norm(resid, gain_row):
    return resid * lax.rsqrt(jnp.mean(resid * resid, axis=1) + eps)[:, None] * gain_row[None, :]


def local(hidden_in, seg_ids, norm_gain, w_z, w_x, w_bc, w_dt, conv_x_w, conv_x_b, conv_bc_w,
          conv_bc_b, dt_bias, a_log, d_skip, gate_gain, w_out, out_cot):
    rows, model = hidden_in.shape
    layers = w_z.shape[0]
    heads = w_dt.shape[2]
    inner = w_z.shape[2]
    state2 = w_bc.shape[2]
    width = state2 // 2
    taps = conv_x_w.shape[1]
    inner_total = inner * lax.axis_size("head")
    seq_bits = bits_of("seq")
    top_down = list(reversed(range(1, seq_bits)))
    orders = ([0] + top_down, top_down + [0], top_down[:1] + [0] + top_down[1:])

    padded = jnp.concatenate(
        [jnp.full((taps - 1,), -1, jnp.int32), seg_ids, jnp.full((taps - 1,), -1, jnp.int32)]
    )
    around = lax.dynamic_slice_in_dim(
        padded, lax.axis_index("seq") * rows, rows + 2 * (taps - 1)
    )
    own = around[taps - 1 : taps - 1 + rows]
    seg_before = around[taps - 2]
    columns = [around[k : k + rows] == own for k in range(taps - 1)]
    columns += [own == own[rows - 1], own == seg_before]
    columns += [around[2 * (taps - 1) - k : 2 * (taps - 1) - k + rows] == own for k in range(taps - 1)]
    aux = jnp.stack(columns, axis=1).astype(F32)
    segc, segr = own[:, None], own[None, :]

    resid = own_piece(hidden_in.astype(F32), "head", 0)
    saved = []
    for l in range(layers):
        if l == 0:
            normed_f = in_norm(hidden_in.astype(F32), norm_gain[l])
        else:
            normed_f = gather_back(in_norm(resid, norm_gain[l]), "head", 0)
        z, x, bc, dtp, nb = run(
            k_proj,
            [((rows, inner), F32), ((rows, inner), F32), ((rows, state2), F32),
             ((rows, heads), F32), ((rows, model), BF)],
            normed_f, w_z, w_x, w_bc, w_dt, blocks={1: l, 2: l, 3: l, 4: l}, name="proj",
        )
        edge = rotate(jnp.concatenate([x[rows - HALO :], bc[rows - HALO :]], 1), "seq", 1)
        ux, ubc, dts, cum, cumt, msg = run(
            functools.partial(k_front, l),
            [((rows, inner), F32), ((rows, state2), F32), ((rows, heads), F32),
             ((rows, heads), F32), ((heads, rows), F32), ((inner + heads, width), F32)],
            x, bc, dtp, edge, aux, conv_x_w, conv_x_b, conv_bc_w, conv_bc_b, dt_bias, a_log,
            blocks={5: l, 7: l},
            scratch=(pltpu.VMEM((rows + HALO, inner), F32), pltpu.VMEM((rows + HALO, state2), F32)),
            name="front",
        )
        inc = carried(msg, heads, False)
        (yp,) = run(
            functools.partial(k_intra, l), [((rows, inner), F32)],
            ux, ubc, dts, cum, cumt, segc, segr, d_skip, name="intra",
        )
        mixed, gated, ss = run(
            k_gate, [((rows, inner), F32), ((rows, inner), F32), ((1, rows), F32)],
            yp, ubc, cum, aux, z, inc, name="gate",
        )
        ss = lax.psum(ss, "head")
        gn, part = run(
            functools.partial(k_out, l, inner_total),
            [((rows, inner), BF), ((rows, model), F32)],
            gated, ss, gate_gain, w_out, blocks={3: l}, name="out",
        )
        branch = scatter_sum(part, "head", 0)
        saved.append((resid, z, x, bc, dtp, nb, edge, ux, ubc, dts, cum, cumt, inc, mixed, gated,
                      ss, gn))
        resid = resid + branch
    (hidden_out,) = run(
        k_round, [((rows, model), BF)], gather_back(resid, "head", 0), flops=1000000, name="round"
    )

    cot_full = out_cot
    cot = own_piece(out_cot, "head", 0)
    wide = [[None] * layers for _ in range(3)]
    narrow = [None] * layers
    small = [None] * layers
    gains = [None] * layers
    for l in reversed(range(layers)):
        (resid, z, x, bc, dtp, nb, edge, ux, ubc, dts, cum, cumt, inc, mixed, gated, ss,
         gn) = saved[l]
        cb, dgn, cross, ggain = run(
            functools.partial(k_b1, l, inner_total),
            [((rows, model), BF), ((rows, inner), F32), ((1, rows), F32), ((1, inner), F32)],
            cot_full, w_out, gated, ss, gate_gain, blocks={1: l}, name="b1",
        )
        cross = lax.psum(cross, "head")
        dm, dz, msg = run(
            functools.partial(k_b2, l, inner_total),
            [((rows, inner), F32), ((rows, inner), BF), ((inner + heads, width), F32)],
            dgn, gated, mixed, z, ss, cross, gate_gain, ubc, cum, cumt, aux, name="b2",
        )
        fin = carried(msg, heads, True)
        dx, dbc, dcum, ddt, gskip = run(
            functools.partial(k_b3, l),
            [((rows, inner), F32), ((rows, state2), F32), ((rows, heads), F32),
             ((rows, heads), F32), ((1, heads), F32)],
            dm, ux, ubc, dts, cum, cumt, segc, segr, mixed, inc, aux, d_skip, name="b3",
        )
        du, dbo, dd, gdtb, galog = run(
            functools.partial(k_b4, l),
            [((rows, inner), F32), ((rows, state2), F32), ((rows, heads), BF),
             ((1, heads), F32), ((1, heads), F32)],
            ux, ubc, dts, dtp, cum, aux, dx, dbc, dcum, ddt, fin, inc, dt_bias, a_log, name="b4",
        )
        halo_x = rotate(du[:HALO], "seq", -1)
        dbq = scatter_sum(dbo, "head", 1)
        dub = dbq * silu_slope(own_piece(ubc, "head", 1))
        halo_b = rotate(dub[:HALO], "seq", -1)
        quarter = dub.shape[1]
        dxb, gcw, gcb = run(
            k_conv_back,
            [((rows, inner), BF), ((taps, inner), F32), ((1, inner), F32)],
            du, halo_x, x, edge[:, :inner], aux, conv_x_w, blocks={5: l},
            scratch=(pltpu.VMEM((rows + HALO, inner), F32), pltpu.VMEM((rows + HALO, inner), F32)),
            name="convx",
        )
        dbb, gbw, gbb = run(
            k_conv_back,
            [((rows, quarter), BF), ((taps, quarter), F32), ((1, quarter), F32)],
            dub, halo_b, own_piece(bc, "head", 1), own_piece(edge[:, inner:], "head", 1), aux,
            own_piece(conv_bc_w[l], "head", 1),
            scratch=(pltpu.VMEM((rows + HALO, quarter), F32),
                     pltpu.VMEM((rows + HALO, quarter), F32)),
            name="convb",
        )
        (part,) = run(
            k_dnorm, [((rows, model), F32)],
            dz, dxb, dd, dbb, w_z, w_x, w_dt, own_piece(w_bc[l], "head", 1),
            blocks={4: l, 5: l, 6: l}, name="dnorm",
        )
        d_normed = scatter_sum(part, "head", 0)
        wide[2][l] = seq_scatter(mm(cb, gn, TN), orders[2])
        wide[0][l] = seq_scatter(mm(nb, dz, TN), orders[0])
        wide[1][l] = seq_scatter(mm(nb, dxb, TN), orders[1])
        narrow[l] = seq_scatter(
            jnp.concatenate([mm(nb, dbb, TN), mm(nb, dd, TN)], axis=1), orders[0]
        )
        _, norm_pull = jax.vjp(in_norm, resid, norm_gain[l])
        d_resid, d_gain = norm_pull(d_normed)
        gains[l] = d_gain
        small[l] = (gcw, gcb, gbw, gbb, gdtb, galog, gskip, ggain)
        cot = cot + d_resid
        cot_full = gather_back(cot, "head", 0)

    flat = [part.reshape(-1) for l in range(layers) for part in small[l]] + gains
    sizes = [part.size for part in flat]
    packed = jnp.concatenate(flat)
    packed = jnp.pad(packed, (0, -packed.size % 1024)).reshape(-1, 128)
    packed = seq_sum(packed).reshape(-1)
    pieces, start = [], 0
    for size in sizes:
        pieces.append(packed[start : start + size])
        start += size
    count = len(small[0])

    def both(slot):
        return jnp.stack([pieces[l * count + slot].reshape(small[l][slot].shape) for l in range(layers)])

    grad_gain = head_sum(jnp.stack(pieces[layers * count :]))
    share = model // lax.axis_size("seq")
    grad_gain = lax.dynamic_slice_in_dim(grad_gain, lax.axis_index("seq") * share, share, 1)
    quarter = state2 // lax.axis_size("head")
    narrow = jnp.stack(narrow)
    bc_parts = jnp.concatenate([narrow[:, :, :quarter], both(2), both(3)], axis=1)
    bc_parts = gather_back(bc_parts, "head", 2)
    return (
        hidden_out,
        cot_full,
        grad_gain,
        jnp.stack(wide[0]),
        jnp.stack(wide[1]),
        bc_parts[:, :share],
        narrow[:, :, quarter:],
        both(0),
        both(1)[:, 0],
        bc_parts[:, share : share + taps],
        bc_parts[:, share + taps],
        both(4)[:, 0],
        both(5)[:, 0],
        both(6)[:, 0],
        both(7)[:, 0],
        jnp.stack([part.T for part in wide[2]]),
    )


def solution(mesh):
    return jax.shard_map(
        local,
        mesh=mesh,
        in_specs=(
            P("seq", None),
            P(),
            P(),
            P(None, None, "head"),
            P(None, None, "head"),
            P(),
            P(None, None, "head"),
            P(None, None, "head"),
            P(None, "head"),
            P(),
            P(),
            P(None, "head"),
            P(None, "head"),
            P(None, "head"),
            P(None, "head"),
            P(None, "head", None),
            P("seq", None),
        ),
        out_specs=(
            P("seq", None),
            P("seq", None),
            P(None, "seq"),
            P(None, "seq", "head"),
            P(None, "seq", "head"),
            P(None, "seq", None),
            P(None, "seq", "head"),
            P(None, None, "head"),
            P(None, "head"),
            P(),
            P(),
            P(None, "head"),
            P(None, "head"),
            P(None, "head"),
            P(None, "head"),
            P(None, "head", "seq"),
        ),
        check_vma=False,
    )
```

time: 1110 us -> 616 us (0.55)
  waiting for transfers between devices: 604 us -> 139 us
  starting transfers between devices: 21.9 us -> 210 us
  blocking collectives: 165 us -> 27.2 us
  matrix products: 117 us -> 9.33 us
  Pallas kernels: 0 us -> 89.3 us
  other arithmetic: 112 us -> 66.5 us
  between operations: 17.3 us -> 2.17 us
    reduce_scatter x5 -> x0, waiting for transfers between devices: 403 us -> none  [the longest x1 92.6 us: local(): lax.psum_scatter(jnp.stack(big_lists[4]), 'seq', scatter_dimension=2, til...]
    ppermute x8 -> x69, starting transfers between devices: 20.9 us -> 210 us  [the longest x63 192 us: swap(): return lax.ppermute(value, axis, [(i, i ^ mask) for i in range(count)])]
    ppermute x8 -> x69, waiting for transfers between devices: 5.26 us -> 139 us  [the longest x63 132 us: swap(): return lax.ppermute(value, axis, [(i, i ^ mask) for i in range(count)])]
    dot_general x64 -> x10, matrix products: 117 us -> 9.33 us  [mm(): lax.dot_general(left, right, (dims, ((), ())), preferred_element_type=F32)]
    psum x3 -> x0, waiting for transfers between devices: 101 us -> none  [the longest x2 74.5 us: local(): lax.psum(jnp.dot(gated_normed, w_out[layer_idx], preferred_element_type=j...]
    all_gather x4 -> x0, waiting for transfers between devices: 95.5 us -> none  [carried_in_2(): gathered = jax.tree.map(lambda a: lax.all_gather(a, axis), part)]
    pallas_call x0 -> x25, Pallas kernels: none -> 89.3 us  [run(): pl.pallas_call(body, grid=(1,), in_specs=in_specs, out_specs=[whole(shape...]
    all_gather x4 -> x0, blocking collectives: 85.3 us -> none  [carried_in_2(): gathered = jax.tree.map(lambda a: lax.all_gather(a, axis), part)]
  transfers between devices with their start and end apart: 21 -> 69, of which waited for: 14 -> 30; matrix products, arithmetic and copies ran while one was open for 10% -> 19% of each run, Pallas kernels for 0% -> 9%
where the time goes in v1:
time: 616 us; the launch traced here: 606 us
  starting transfers between devices  210 us (34%)
  waiting for transfers between devices  139 us (23%)
  Pallas kernels  89.3 us (14%)
  other arithmetic  66.5 us (11%)
  local copies, waits for them, and re-layouts  62.9 us (10%)
  blocking collectives  27.2 us (4%)
  matrix products  9.33 us (2%)
    ppermute x63, starting transfers between devices, swap(): return lax.ppermute(value, axis, [(i, i ^ mask) for i in range(count)])  192 us
    ppermute x63, waiting for transfers between devices, swap(): return lax.ppermute(value, axis, [(i, i ^ mask) for i in range(count)])  132 us
    pallas_call x25, Pallas kernels, run(): pl.pallas_call(body, grid=(1,), in_specs=in_specs, out_specs=[whole(shape...  89.3 us
    dynamic_slice x35, local copies, waits for them, and re-layouts, halves(): send = lax.dynamic_slice_in_dim(value, (1 - which) * half, half, dim)  21.2 us
    unnamed x158, local copies, waits for them, and re-layouts  20.2 us
    ppermute x6, starting transfers between devices, rotate(): lax.ppermute(value, axis, [(i, (i + steps) % count) for i in range(count)])  17.9 us
    psum x2, blocking collectives, local(): cross = lax.psum(cross, 'head')  14.6 us
    add x18, other arithmetic, seq_scatter(): value = keep + swap(send, 'seq', mask_of(bit))  12.7 us
  transfers between devices with their start and end apart: 69, of which 30 were waited for; matrix products, arithmetic and copies ran while one was open for 19% of the time, Pallas kernels for 9%

profile of v1, /device:TPU:0, one launch (start us, length us, event | category | flops | bytes accessed | tf_op | source)
XLA Modules:
  0.0 606.2 jit_solution(354819341092385780)
XLA Ops:
  24.3 7.5 %collective-permute-done.1 = f32[520,128]{1,0:T(8,128)S(1)} collective-permute-done((f32[520,128]{1,0:T(8,128)}, f32[520,128]{1,0:T(8,128)S(1)}, u32[]{:S(2)}, u32[]{:S(2)}) %collective-permute-start.1) | collective-permute-done | bytes 266272 | tf_op jit(solution)/shard_map/ppermute | solution.py:18
  34.0 6.0 collective-permute-done.2
  52.4 6.3 %psum.28.ss = f32[1,256]{1,0:T(1,128)} all-reduce(f32[1,256]{1,0:T(1,128)} %get-tuple-element.105), channel_id=1, replica_groups=mesh['seq'=8,'head'=4] {'head'}, use_global_device_ids=true, to_apply=%region_1.2 | all-reduce | flops 256 | bytes 2048 | tf_op jit(solution)/shard_map/psum | solution.py:544
  67.8 6.5 %collective-permute-done.5 = f32[64,1024]{1,0:T(8,128)S(1)} collective-permute-done((f32[64,1024]{1,0:T(8,128)S(1)}, f32[64,1024]{1,0:T(8,128)S(1)}, u32[]{:S(2)}, u32[]{:S(2)}) %collective-permute-start.5) | collective-permute-done | bytes 262176 | tf_op jit(solution)/shard_map/ppermute | solution.py:18
  76.4 5.8 collective-permute-done.6
  94.1 5.2 collective-permute-done.8.edge
  134.2 6.3 %psum.29.ss = f32[1,256]{1,0:T(1,128)} all-reduce(f32[1,256]{1,0:T(1,128)} %get-tuple-element.118), channel_id=1, replica_groups=mesh['seq'=8,'head'=4] {'head'}, use_global_device_ids=true, to_apply=%region_3.4 | all-reduce | flops 256 | bytes 2048 | tf_op jit(solution)/shard_map/psum | solution.py:544
  146.7 7.8 %psum.30.cross = f32[1,256]{1,0:T(1,128)} all-reduce(f32[1,256]{1,0:T(1,128)} %get-tuple-element.122), channel_id=1, replica_groups=mesh['seq'=8,'head'=4] {'head'}, use_global_device_ids=true, to_apply=%region_4.5 | all-reduce | flops 256 | bytes 2048 | tf_op jit(solution)/shard_map/psum | solution.py:572
  166.2 4.8 collective-permute-start.17
  171.4 6.4 %b3.2 = (f32[256,512]{1,0:T(8,128)}, f32[256,256]{1,0:T(8,128)}, f32[256,8]{1,0:T(8,128)}, f32[256,8]{1,0:T(8,128)}, f32[1,8]{1,0:T(1,128)}) custom-call(f32[256,512]{1,0:T(8,128)} %get-tuple-element.124.dm, f32[256,512]{1,0:T(8,128)} %get-tuple-element.110.ux, f32[256,256]{1,0:T(8,128)} %get-tuple-element.111.ubc, f32[256,8]{1,0:T(8,128)} %get-tuple-element.112.dts, ...), custom_call_target="tpu_custom_call" | custom-call | flops 2000000000 | bytes 2132032 | tf_op jit(solution)/shard_map/b3/pallas_call | solution.py:213
  189.6 4.1 b4.2
  227.9 6.6 %collective-permute-done.58 = f32[2,2,1,128,72]{4,3,2,1,0:T(8,128)S(1)} collective-permute-done((f32[2,2,1,128,72]{4,3,2,1,0:T(8,128)S(1)}, f32[2,2,1,128,72]{4,3,2,1,0:T(8,128)S(1)}, u32[]{:S(2)}, u32[]{:S(2)}) %collective-permute-start.58) | collective-permute-done | bytes 147488 | tf_op jit(solution)/shard_map/ppermute | solution.py:18
  242.6 35.4 %collective-permute-start.60 = (f32[1,1,1,128,72]{4,3,2,1,0:T(8,128)S(1)}, f32[1,1,1,128,72]{4,3,2,1,0:T(8,128)S(1)}, u32[]{:S(2)}, u32[]{:S(2)}) collective-permute-start(f32[1,1,1,128,72]{4,3,2,1,0:T(8,128)S(1)} %constant_dynamic-slice_fusion.9), channel_id=1, source_target_pairs={{0,8},{4,12},{8,0},{12,4},{16,24},{20,28},{24,16},{28,20},{1,9},{5... | collective-permute-start | bytes 110600 | tf_op jit(solution)/shard_map/ppermute | solution.py:18
  280.8 7.4 %collective-permute-start.48 = (f32[1,1,1,128,512]{4,3,2,1,0:T(8,128)S(1)}, f32[1,1,1,128,512]{4,3,2,1,0:T(8,128)S(1)}, u32[]{:S(2)}, u32[]{:S(2)}) collective-permute-start(f32[1,1,1,128,512]{4,3,2,1,0:T(8,128)S(1)} %constant_dynamic-slice_fusion.21), channel_id=1, source_target_pairs={{0,8},{4,12},{8,0},{12,4},{16,24},{20,28},{24,16},{28,20},{1,9},{5... | collective-permute-start | bytes 786440 | tf_op jit(solution)/shard_map/ppermute | solution.py:18
  293.9 5.3 collective-permute-done.25
  312.1 6.8 %psum.31.cross = f32[1,256]{1,0:T(1,128)} all-reduce(f32[1,256]{1,0:T(1,128)} %get-tuple-element.137), channel_id=1, replica_groups=mesh['seq'=8,'head'=4] {'head'}, use_global_device_ids=true, to_apply=%region_6.7 | all-reduce | flops 256 | bytes 2048 | tf_op jit(solution)/shard_map/psum | solution.py:572
  327.4 4.4 collective-permute-done.27
  346.1 6.5 %b3.3 = (f32[256,512]{1,0:T(8,128)}, f32[256,256]{1,0:T(8,128)}, f32[256,8]{1,0:T(8,128)}, f32[256,8]{1,0:T(8,128)}, f32[1,8]{1,0:T(1,128)}) custom-call(f32[256,512]{1,0:T(8,128)} %get-tuple-element.139.dm, f32[256,512]{1,0:T(8,128)} %get-tuple-element.97.ux, f32[256,256]{1,0:T(8,128)} %get-tuple-element.98.ubc, f32[256,8]{1,0:T(8,128)} %get-tuple-element.99.dts, ...), custom_call_target="tpu_custom_call" | custom-call | flops 2000000000 | bytes 2132032 | tf_op jit(solution)/shard_map/b3/pallas_call | solution.py:213
  364.8 30.4 %collective-permute-done.29 = f32[520,128]{1,0:T(8,128)S(1)} collective-permute-done((f32[520,128]{1,0:T(8,128)S(1)}, f32[520,128]{1,0:T(8,128)S(1)}, u32[]{:S(2)}, u32[]{:S(2)}) %collective-permute-start.29) | collective-permute-done | bytes 266272 | tf_op jit(solution)/shard_map/ppermute | solution.py:18
  396.9 4.1 b4.3
  422.7 47.1 %collective-permute-start.49 = (f32[1,2,2,128,512]{4,3,2,1,0:T(8,128)}, f32[1,2,2,128,512]{4,3,2,1,0:T(8,128)}, u32[]{:S(2)}, u32[]{:S(2)}) collective-permute-start(f32[1,2,2,128,512]{4,3,2,1,0:T(8,128)} %constant_dynamic-slice_fusion.20), channel_id=1, source_target_pairs={{0,24},{4,28},{8,16},{12,20},{16,8},{20,12},{24,0},{28,4},{1,25},{... | collective-permute-start | bytes 3145736 | tf_op jit(solution)/shard_map/ppermute | solution.py:18
  492.6 12.9 %collective-permute-done.56 = f32[1,2,1,128,72]{4,3,2,1,0:T(8,128)S(1)} collective-permute-done((f32[1,2,1,128,72]{4,3,2,1,0:T(8,128)S(1)}, f32[1,2,1,128,72]{4,3,2,1,0:T(8,128)S(1)}, u32[]{:S(2)}, u32[]{:S(2)}) %collective-permute-start.56) | collective-permute-done | bytes 73760 | tf_op jit(solution)/shard_map/ppermute | solution.py:18
  505.5 35.7 %collective-permute-start.57 = (f32[1,1,1,128,72]{4,3,2,1,0:T(8,128)S(1)}, f32[1,1,1,128,72]{4,3,2,1,0:T(8,128)S(1)}, u32[]{:S(2)}, u32[]{:S(2)}) collective-permute-start(f32[1,1,1,128,72]{4,3,2,1,0:T(8,128)S(1)} %constant_dynamic-slice_fusion.12), channel_id=1, source_target_pairs={{0,8},{4,12},{8,0},{12,4},{16,24},{20,28},{24,16},{28,20},{1,9},{5... | collective-permute-start | bytes 110600 | tf_op jit(solution)/shard_map/ppermute | solution.py:18
  598.4 6.7 %collective-permute-done.51 = f32[1,1,1,128,512]{4,3,2,1,0:T(8,128)S(1)} collective-permute-done((f32[1,1,1,128,512]{4,3,2,1,0:T(8,128)S(1)}, f32[1,1,1,128,512]{4,3,2,1,0:T(8,128)S(1)}, u32[]{:S(2)}, u32[]{:S(2)}) %collective-permute-start.51) | collective-permute-done | bytes 262176 | tf_op jit(solution)/shard_map/ppermute | solution.py:18
  (516 shorter events, 328.4 us)
Async XLA Ops:
  159.6 22.6 %collective-permute-start.12 = (f32[128,1024]{1,0:T(8,128)}, f32[128,1024]{1,0:T(8,128)}, u32[]{:S(2)}, u32[]{:S(2)}) collective-permute-start(f32[128,1024]{1,0:T(8,128)} %constant_dynamic-slice_fusion.43), channel_id=1, source_target_pairs={{0,1},{1,0},{2,3},{3,2},{4,5},{5,4},{6,7},{7,6},{8,9},{9,8},{10,11... | collective-permute-start | bytes 1572872 | tf_op jit(solution)/shard_map/ppermute | solution.py:18
  162.3 63.9 %collective-permute-start.46 = (f32[2,2,1,128,512]{4,3,2,1,0:T(8,128)}, f32[2,2,1,128,512]{4,3,2,1,0:T(8,128)}, u32[]{:S(2)}, u32[]{:S(2)}) collective-permute-start(f32[2,2,1,128,512]{4,3,2,1,0:T(8,128)} %constant_dynamic-slice_fusion.23), channel_id=1, source_target_pairs={{0,4},{4,0},{8,12},{12,8},{16,20},{20,16},{24,28},{28,24},{1,5},{5... | collective-permute-start | bytes 3145736 | tf_op jit(solution)/shard_map/ppermute | solution.py:18
  185.0 103.4 %collective-permute-start.13 = (f32[64,1024]{1,0:T(8,128)}, f32[64,1024]{1,0:T(8,128)}, u32[]{:S(2)}, u32[]{:S(2)}) collective-permute-start(f32[64,1024]{1,0:T(8,128)} %constant_dynamic-slice_fusion.42), channel_id=1, source_target_pairs={{0,2},{1,3},{2,0},{3,1},{4,6},{5,7},{6,4},{7,5},{8,10},{9,11},{10,... | collective-permute-start | bytes 786440 | tf_op jit(solution)/shard_map/ppermute | solution.py:18
  213.9 78.1 %collective-permute-start.52 = (f32[1,2,2,128,512]{4,3,2,1,0:T(8,128)}, f32[1,2,2,128,512]{4,3,2,1,0:T(8,128)}, u32[]{:S(2)}, u32[]{:S(2)}) collective-permute-start(f32[1,2,2,128,512]{4,3,2,1,0:T(8,128)} %constant_dynamic-slice_fusion.17), channel_id=1, source_target_pairs={{0,24},{4,28},{8,16},{12,20},{16,8},{20,12},{24,0},{28,4},{1,25},{... | collective-permute-start | bytes 3145736 | tf_op jit(solution)/shard_map/ppermute | solution.py:18
  224.6 53.5 %collective-permute-start.23 = (f32[128,1024]{1,0:T(8,128)}, f32[128,1024]{1,0:T(8,128)}, u32[]{:S(2)}, u32[]{:S(2)}) collective-permute-start(f32[128,1024]{1,0:T(8,128)} %constant_dynamic-slice_fusion.36), channel_id=1, source_target_pairs={{0,1},{1,0},{2,3},{3,2},{4,5},{5,4},{6,7},{7,6},{8,9},{9,8},{10,11... | collective-permute-start | bytes 1572872 | tf_op jit(solution)/shard_map/ppermute | solution.py:18
  236.5 44.1 %collective-permute-start.47 = (f32[1,2,1,128,512]{4,3,2,1,0:T(8,128)S(1)}, f32[1,2,1,128,512]{4,3,2,1,0:T(8,128)S(1)}, u32[]{:S(2)}, u32[]{:S(2)}) collective-permute-start(f32[1,2,1,128,512]{4,3,2,1,0:T(8,128)S(1)} %constant_dynamic-slice_fusion.22), channel_id=1, source_target_pairs={{0,24},{4,28},{8,16},{12,20},{16,8},{20,12},{24,0},{28,4},{1,25},{... | collective-permute-start | bytes 1572872 | tf_op jit(solution)/shard_map/ppermute | solution.py:18
  242.6 51.1 %collective-permute-start.60 = (f32[1,1,1,128,72]{4,3,2,1,0:T(8,128)S(1)}, f32[1,1,1,128,72]{4,3,2,1,0:T(8,128)S(1)}, u32[]{:S(2)}, u32[]{:S(2)}) collective-permute-start(f32[1,1,1,128,72]{4,3,2,1,0:T(8,128)S(1)} %constant_dynamic-slice_fusion.9), channel_id=1, source_target_pairs={{0,8},{4,12},{8,0},{12,4},{16,24},{20,28},{24,16},{28,20},{1,9},{5... | collective-permute-start | bytes 110600 | tf_op jit(solution)/shard_map/ppermute | solution.py:18
  280.8 18.5 %collective-permute-start.48 = (f32[1,1,1,128,512]{4,3,2,1,0:T(8,128)S(1)}, f32[1,1,1,128,512]{4,3,2,1,0:T(8,128)S(1)}, u32[]{:S(2)}, u32[]{:S(2)}) collective-permute-start(f32[1,1,1,128,512]{4,3,2,1,0:T(8,128)S(1)} %constant_dynamic-slice_fusion.21), channel_id=1, source_target_pairs={{0,8},{4,12},{8,0},{12,4},{16,24},{20,28},{24,16},{28,20},{1,9},{5... | collective-permute-start | bytes 786440 | tf_op jit(solution)/shard_map/ppermute | solution.py:18
  304.6 52.5 %collective-permute-start.15 = (f32[128,1024]{1,0:T(8,128)}, f32[128,1024]{1,0:T(8,128)}, u32[]{:S(2)}, u32[]{:S(2)}) collective-permute-start(f32[128,1024]{1,0:T(8,128)} %maximum_select_fusion.5), channel_id=1, source_target_pairs={{0,1},{1,0},{2,3},{3,2},{4,5},{5,4},{6,7},{7,6},{8,9},{9,8},{10,11... | collective-permute-start | bytes 1572872 | tf_op jit(solution)/shard_map/ppermute | solution.py:18
  307.7 55.4 %collective-permute-start.54 = (f32[1,1,1,128,512]{4,3,2,1,0:T(8,128)}, f32[1,1,1,128,512]{4,3,2,1,0:T(8,128)}, u32[]{:S(2)}, u32[]{:S(2)}) collective-permute-start(f32[1,1,1,128,512]{4,3,2,1,0:T(8,128)} %constant_dynamic-slice_fusion.15), channel_id=1, source_target_pairs={{0,4},{4,0},{8,12},{12,8},{16,20},{20,16},{24,28},{28,24},{1,5},{5... | collective-permute-start | bytes 786440 | tf_op jit(solution)/shard_map/ppermute | solution.py:18
  326.7 152.7 %collective-permute-start.43 = (f32[2,2,1,128,512]{4,3,2,1,0:T(8,128)}, f32[2,2,1,128,512]{4,3,2,1,0:T(8,128)}, u32[]{:S(2)}, u32[]{:S(2)}) collective-permute-start(f32[2,2,1,128,512]{4,3,2,1,0:T(8,128)} %constant_dynamic-slice_fusion.26), channel_id=1, source_target_pairs={{0,4},{4,0},{8,12},{12,8},{16,20},{20,16},{24,28},{28,24},{1,5},{5... | collective-permute-start | bytes 3145736 | tf_op jit(solution)/shard_map/ppermute | solution.py:18
  333.3 19.3 %collective-permute-start.28 = (f32[520,128]{1,0:T(8,128)}, f32[520,128]{1,0:T(8,128)}, u32[]{:S(2)}, u32[]{:S(2)}) collective-permute-start(f32[520,128]{1,0:T(8,128)} %pad_maximum_fusion.11), channel_id=1, source_target_pairs={{0,8},{4,12},{8,0},{12,4},{16,24},{20,28},{24,16},{28,20},{1,9},{5... | collective-permute-start | bytes 798728 | tf_op jit(solution)/shard_map/ppermute | solution.py:18
  342.4 141.0 %collective-permute-start.66 = (f32[1,2,2,128,512]{3,4,2,1,0:T(8,128)}, f32[1,2,2,128,512]{3,4,2,1,0:T(8,128)}, u32[]{:S(2)}, u32[]{:S(2)}) collective-permute-start(f32[1,2,2,128,512]{3,4,2,1,0:T(8,128)} %copy.103), channel_id=1, source_target_pairs={{0,24},{4,28},{8,16},{12,20},{16,8},{20,12},{24,0},{28,4},{1,25},{... | collective-permute-start | bytes 3145736 | tf_op jit(solution)/shard_map/ppermute | solution.py:18
  352.6 137.1 %collective-permute-start.63 = (f32[1,2,2,128,512]{3,4,2,1,0:T(8,128)}, f32[1,2,2,128,512]{3,4,2,1,0:T(8,128)}, u32[]{:S(2)}, u32[]{:S(2)}) collective-permute-start(f32[1,2,2,128,512]{3,4,2,1,0:T(8,128)} %copy.101), channel_id=1, source_target_pairs={{0,24},{4,28},{8,16},{12,20},{16,8},{20,12},{24,0},{28,4},{1,25},{... | collective-permute-start | bytes 3145736 | tf_op jit(solution)/shard_map/ppermute | solution.py:18
  357.1 38.0 %collective-permute-start.29 = (f32[520,128]{1,0:T(8,128)S(1)}, f32[520,128]{1,0:T(8,128)S(1)}, u32[]{:S(2)}, u32[]{:S(2)}) collective-permute-start(f32[520,128]{1,0:T(8,128)S(1)} %pad_maximum_fusion.12), channel_id=1, source_target_pairs={{0,24},{4,28},{8,16},{12,20},{16,8},{20,12},{24,0},{28,4},{1,25},{... | collective-permute-start | bytes 798728 | tf_op jit(solution)/shard_map/ppermute | solution.py:18
  417.2 52.6 %collective-permute-start.33 = (f32[8,64]{1,0:T(8,128)S(1)}, f32[8,64]{1,0:T(8,128)S(1)}, u32[]{:S(2)}, u32[]{:S(2)}) collective-permute-start(f32[8,64]{1,0:T(8,128)S(1)} %slice.346), channel_id=1, source_target_pairs={{0,28},{4,0},{8,4},{12,8},{16,12},{20,16},{24,20},{28,24},{1,29},{... | collective-permute-start | bytes 6152 | tf_op jit(solution)/shard_map/ppermute | solution.py:23
  422.7 157.7 %collective-permute-start.49 = (f32[1,2,2,128,512]{4,3,2,1,0:T(8,128)}, f32[1,2,2,128,512]{4,3,2,1,0:T(8,128)}, u32[]{:S(2)}, u32[]{:S(2)}) collective-permute-start(f32[1,2,2,128,512]{4,3,2,1,0:T(8,128)} %constant_dynamic-slice_fusion.20), channel_id=1, source_target_pairs={{0,24},{4,28},{8,16},{12,20},{16,8},{20,12},{24,0},{28,4},{1,25},{... | collective-permute-start | bytes 3145736 | tf_op jit(solution)/shard_map/ppermute | solution.py:18
  478.1 71.3 %collective-permute-start.34 = (f32[128,1024]{1,0:T(8,128)}, f32[128,1024]{1,0:T(8,128)}, u32[]{:S(2)}, u32[]{:S(2)}) collective-permute-start(f32[128,1024]{1,0:T(8,128)} %constant_dynamic-slice_fusion.29), channel_id=1, source_target_pairs={{0,1},{1,0},{2,3},{3,2},{4,5},{5,4},{6,7},{7,6},{8,9},{9,8},{10,11... | collective-permute-start | bytes 1572872 | tf_op jit(solution)/shard_map/ppermute | solution.py:18
  483.4 69.3 %collective-permute-start.44 = (f32[1,2,1,128,512]{4,3,2,1,0:T(8,128)}, f32[1,2,1,128,512]{4,3,2,1,0:T(8,128)}, u32[]{:S(2)}, u32[]{:S(2)}) collective-permute-start(f32[1,2,1,128,512]{4,3,2,1,0:T(8,128)} %constant_dynamic-slice_fusion.25), channel_id=1, source_target_pairs={{0,24},{4,28},{8,16},{12,20},{16,8},{20,12},{24,0},{28,4},{1,25},{... | collective-permute-start | bytes 1572872 | tf_op jit(solution)/shard_map/ppermute | solution.py:18
  488.2 17.3 %collective-permute-start.56 = (f32[1,2,1,128,72]{4,3,2,1,0:T(8,128)S(1)}, f32[1,2,1,128,72]{4,3,2,1,0:T(8,128)S(1)}, u32[]{:S(2)}, u32[]{:S(2)}) collective-permute-start(f32[1,2,1,128,72]{4,3,2,1,0:T(8,128)S(1)} %constant_dynamic-slice_fusion.13), channel_id=1, source_target_pairs={{0,24},{4,28},{8,16},{12,20},{16,8},{20,12},{24,0},{28,4},{1,25},{... | collective-permute-start | bytes 221192 | tf_op jit(solution)/shard_map/ppermute | solution.py:18
  489.6 67.1 %collective-permute-start.67 = (f32[1,2,1,128,512]{3,4,2,1,0:T(8,128)}, f32[1,2,1,128,512]{3,4,2,1,0:T(8,128)}, u32[]{:S(2)}, u32[]{:S(2)}) collective-permute-start(f32[1,2,1,128,512]{3,4,2,1,0:T(8,128)} %constant_dynamic-slice_fusion.2), channel_id=1, source_target_pairs={{0,4},{4,0},{8,12},{12,8},{16,20},{20,16},{24,28},{28,24},{1,5},{5... | collective-permute-start | bytes 1572872 | tf_op jit(solution)/shard_map/ppermute | solution.py:18
  505.5 37.9 %collective-permute-start.57 = (f32[1,1,1,128,72]{4,3,2,1,0:T(8,128)S(1)}, f32[1,1,1,128,72]{4,3,2,1,0:T(8,128)S(1)}, u32[]{:S(2)}, u32[]{:S(2)}) collective-permute-start(f32[1,1,1,128,72]{4,3,2,1,0:T(8,128)S(1)} %constant_dynamic-slice_fusion.12), channel_id=1, source_target_pairs={{0,8},{4,12},{8,0},{12,4},{16,24},{20,28},{24,16},{28,20},{1,9},{5... | collective-permute-start | bytes 110600 | tf_op jit(solution)/shard_map/ppermute | solution.py:18
  554.7 18.1 %collective-permute-start.45 = (f32[1,1,1,128,512]{4,3,2,1,0:T(8,128)}, f32[1,1,1,128,512]{4,3,2,1,0:T(8,128)}, u32[]{:S(2)}, u32[]{:S(2)}) collective-permute-start(f32[1,1,1,128,512]{4,3,2,1,0:T(8,128)} %constant_dynamic-slice_fusion.24), channel_id=1, source_target_pairs={{0,8},{4,12},{8,0},{12,4},{16,24},{20,28},{24,16},{28,20},{1,9},{5... | collective-permute-start | bytes 786440 | tf_op jit(solution)/shard_map/ppermute | solution.py:18
  571.9 21.4 %collective-permute-start.36 = (f32[64,1024]{1,0:T(8,128)}, f32[64,1024]{1,0:T(8,128)}, u32[]{:S(2)}, u32[]{:S(2)}) collective-permute-start(f32[64,1024]{1,0:T(8,128)} %fusion.1), channel_id=1, source_target_pairs={{0,2},{1,3},{2,0},{3,1},{4,6},{5,7},{6,4},{7,5},{8,10},{9,11},{10,... | collective-permute-start | bytes 786440 | tf_op jit(solution)/shard_map/ppermute | solution.py:18
  (121 other events, 1294.2 us)

commit v2 on v1

--- a/solution.py
+++ b/solution.py
@@ -11,6 +11,7 @@
 F32, BF = jnp.float32, jnp.bfloat16
 NN, NT, TN = ((1,), (0,)), ((1,), (1,)), ((0,), (0,))
 HALO = 8
+GRANT = 24 << 20
 
 
 def swap(value, axis, mask):
@@ -31,18 +32,42 @@
     return lax.axis_size(axis).bit_length() - 1
 
 
-def halves(value, which, dim):
-    half = value.shape[dim] // 2
-    keep = lax.dynamic_slice_in_dim(value, which * half, half, dim)
-    send = lax.dynamic_slice_in_dim(value, (1 - which) * half, half, dim)
-    return keep, send
-
-
-def scatter_sum(value, axis, dim):
+def reverse_bits(value, count):
+    result = 0
+    for bit in range(count):
+        result = result | (((value >> bit) & 1) << (count - 1 - bit))
+    return result
+
+
+def relative_order(count):
+    return [reverse_bits(i, count) for i in range(1 << count)]
+
+
+def finish_scatter(keep, send, axis):
     for bit in range(bits_of(axis)):
-        keep, send = halves(value, bit_of(axis, bit), dim)
+        got = swap(send, axis, 1 << bit)
+        half = keep.shape[0] // 2
+        if bit + 1 < bits_of(axis):
+            send = keep[half:] + got[half:]
+            keep = keep[:half] + got[:half]
+    return keep, got
+
+
+def scatter_cols(value, axis):
+    for bit in range(bits_of(axis)):
+        half = value.shape[1] // 2
+        which = bit_of(axis, bit)
+        keep = lax.dynamic_slice_in_dim(value, which * half, half, 1)
+        send = lax.dynamic_slice_in_dim(value, (1 - which) * half, half, 1)
         value = keep + swap(send, axis, 1 << bit)
     return value
+
+
+def gather_pieces(mine, axis):
+    pieces = [mine]
+    for bit in reversed(range(bits_of(axis))):
+        pieces = pieces + [swap(piece, axis, 1 << bit) for piece in pieces]
+    return pieces
 
 
 def gather_back(value, axis, dim):
@@ -68,20 +93,30 @@
     return 1 << bit if bit < 2 else 3 << (bit - 1)
 
 
-def seq_scatter(value, order):
-    count = bits_of("seq")
-    rows, cols = value.shape
-    value = value.reshape((2,) * count + (rows >> count, cols))
-    top = list(reversed(range(count)))
+def seq_places(order, share):
+    count = len(order)
+    me = lax.axis_index("seq")
+    starts = []
+    for piece in range(1 << count):
+        mask = 0
+        for step, bit in enumerate(order):
+            if (piece >> (count - 1 - step)) & 1:
+                mask ^= mask_of(bit)
+        starts.append((me ^ mask) * share)
+    return jnp.stack(starts).astype(jnp.int32)
+
+
+def seq_step(keep, send, bit, last, after=()):
+    got = swap(send, "seq", mask_of(bit))
+    rows, cols = keep.shape
+    if last:
+        return keep + got, None
+    half = ((rows // 2, cols), F32)
+    return run(k_add, [half, half], keep, got, after=after, flops=rows * cols, name="add")
+
+
+def seq_sum(value, order):
     for bit in order:
-        dim = top.index(bit)
-        keep, send = halves(value, bit_of("seq", bit), dim)
-        value = keep + swap(send, "seq", mask_of(bit))
-    return value.reshape(rows >> count, cols)
-
-
-def seq_sum(value):
-    for bit in range(bits_of("seq")):
         value = value + swap(value, "seq", mask_of(bit))
     return value
 
@@ -93,27 +128,26 @@
 
 
 def carried(message, heads, reverse):
-    cols = message.shape[1]
-    rows = message.shape[0] - heads
-    state = message[:rows].reshape(heads, rows // heads, cols)
-    decay = message[rows:].reshape(heads, 1, cols)
-    ahead_s, ahead_d = jnp.zeros_like(state), jnp.ones_like(decay)
     count = bits_of("seq")
-    for bit in range(count):
-        packed = jnp.concatenate([state.reshape(rows, cols), decay.reshape(heads, cols)], 0)
-        got = swap(packed, "seq", mask_of(bit))
-        got_s = got[:rows].reshape(heads, rows // heads, cols)
-        got_d = got[rows:].reshape(heads, 1, cols)
-        upper = bit_of("seq", bit) == 1
-        later = jnp.logical_not(upper) if reverse else upper
-        ahead_s, ahead_d = (
-            jnp.where(later, ahead_d * got_s + ahead_s, ahead_s),
-            jnp.where(later, ahead_d * got_d, ahead_d),
-        )
-        if bit + 1 < count:
-            state = jnp.where(later, decay * got_s + state, got_d * state + got_s)
-            decay = decay * got_d
-    return ahead_s.reshape(rows, cols)
+    shape = [(message.shape, F32)]
+    flags = [
+        ((1 - bit_of("seq", bit)) if reverse else bit_of("seq", bit)).reshape(1).astype(jnp.int32)
+        for bit in range(count)
+    ]
+    ahead = None
+    for bit in range(count - 1):
+        got = swap(message, "seq", mask_of(bit))
+        if ahead is None:
+            ahead, message = run(
+                functools.partial(k_scan_first, heads), shape * 2, message, got, small=[flags[bit]],
+                flops=1000000, name="scan",
+            )
+        else:
+            ahead, message = run(
+                functools.partial(k_scan, heads), shape * 2, message, ahead, got,
+                small=[flags[bit]], flops=1000000, name="scan",
+            )
+    return ahead, swap(message, "seq", mask_of(count - 1)), flags[count - 1]
 
 
 def mm(left, right, dims):
@@ -191,44 +225,137 @@
     return sig * (1.0 + value * (1.0 - sig))
 
 
-def run(body, outs, *args, blocks=None, scratch=(), flops=2_000_000_000, name=None):
-    blocks = blocks or {}
-
-    def whole(shape):
-        return pl.BlockSpec(shape, lambda i: (0,) * len(shape))
-
-    in_specs = []
-    for place, arg in enumerate(args):
-        if place in blocks:
-            layer = blocks[place]
-            in_specs.append(
-                pl.BlockSpec(
-                    (pl.Squeezed(),) + arg.shape[1:],
-                    functools.partial(lambda l, n, i: (l,) + (0,) * n, layer, arg.ndim - 1),
-                )
-            )
-        else:
-            in_specs.append(whole(arg.shape))
-    moved = sum(a.size * a.dtype.itemsize for a in args)
+class Far:
+    def __init__(self, value, layer=None):
+        self.value, self.layer = value, layer
+        self.shape = value.shape if layer is None else value.shape[1:]
+
+
+def run(body, outs, *args, small=(), after=(), scratch=(), flops=2_000_000_000, name=None):
+    held = pl.BlockSpec(memory_space=pltpu.VMEM)
+    first, second = len(small), len(small) + len(args)
+    far = [i for i, arg in enumerate(args) if isinstance(arg, Far)]
+    layers = [arg.layer if isinstance(arg, Far) else None for arg in args]
+    values = [arg.value if isinstance(arg, Far) else arg for arg in args]
+    buffers = [pltpu.VMEM(args[i].shape, values[i].dtype) for i in far]
+    if far:
+        buffers = buffers + [pltpu.SemaphoreType.DMA((len(far),))]
+    moved = sum(a.size * a.dtype.itemsize for a in values)
+
+    def inner(*refs):
+        given = list(refs[:second])
+        rest = refs[second + len(after) :]
+        if far:
+            rest, fetched, sem = rest[: -len(far) - 1], rest[-len(far) - 1 : -1], rest[-1]
+            copies = []
+            for slot, i in enumerate(far):
+                source = given[first + i]
+                source = source if layers[i] is None else source.at[layers[i]]
+                copies.append(pltpu.make_async_copy(source, fetched[slot], sem.at[slot]))
+                given[first + i] = fetched[slot]
+            for copy in copies:
+                copy.start()
+            for copy in copies:
+                copy.wait()
+        body(*given, *rest)
+
     return pl.pallas_call(
-        body,
-        grid=(1,),
-        in_specs=in_specs,
-        out_specs=[whole(shape) for shape, kind in outs],
+        inner,
+        in_specs=[pl.BlockSpec(memory_space=pltpu.SMEM)] * first
+        + [pl.BlockSpec(memory_space=pltpu.HBM) if i in far else held for i in range(len(args))]
+        + [pl.BlockSpec(memory_space=pl.ANY)] * len(after),
+        out_specs=[held] * len(outs),
         out_shape=[jax.ShapeDtypeStruct(shape, kind) for shape, kind in outs],
-        scratch_shapes=list(scratch),
+        scratch_shapes=list(scratch) + buffers,
+        compiler_params=pltpu.CompilerParams(vmem_limit_bytes=GRANT),
         cost_estimate=pl.CostEstimate(flops=flops, bytes_accessed=moved, transcendentals=0),
         name=name,
-    )(*args)
-
-
-def k_proj(xn, wz, wx, wbc, wdt, z, x, bc, dt, nb):
-    rounded = xn[...].astype(BF)
-    nb[...] = rounded
+    )(*small, *values, *after)
+
+
+def rows_at(place, piece, size):
+    return pl.ds(pl.multiple_of(place[piece], size), size)
+
+
+def norm_rows(value, gain):
+    return value * lax.rsqrt(jnp.mean(value * value, axis=1, keepdims=True) + eps) * gain
+
+
+def k_add(keep, got, first, second):
+    half = first.shape[0]
+    first[...] = keep[0:half, :] + got[0:half, :]
+    second[...] = keep[half:, :] + got[half:, :]
+
+
+def merge(heads, flag, near, far, state, decay=None):
+    rows = near.shape[0] - heads
+    per = rows // heads
+    use = flag[0] == 1
+    for head in range(heads):
+        cols = slice(head * per, (head + 1) * per)
+        fade = near[rows + head : rows + head + 1, :]
+        state[cols, :] = jnp.where(use, fade * far[cols, :] + near[cols, :], near[cols, :])
+    if decay is not None:
+        fades = near[rows:, :]
+        decay[...] = jnp.where(use, fades * far[rows:, :], fades)
+
+
+def k_scan_first(heads, flag, mine, got, ahead, total):
+    rows = mine.shape[0] - heads
+    use = flag[0] == 1
+    ahead[0:rows, :] = jnp.where(use, got[0:rows, :], 0.0)
+    ahead[rows:, :] = jnp.where(use, got[rows:, :], 1.0)
+    join(heads, use, mine, got, total)
+
+
+def join(heads, use, mine, got, total):
+    rows = mine.shape[0] - heads
+    per = rows // heads
+    for head in range(heads):
+        cols = slice(head * per, (head + 1) * per)
+        own, other = mine[cols, :], got[cols, :]
+        own_fade = mine[rows + head : rows + head + 1, :]
+        got_fade = got[rows + head : rows + head + 1, :]
+        total[cols, :] = jnp.where(use, own_fade * other + own, got_fade * own + other)
+    total[rows:, :] = mine[rows:, :] * got[rows:, :]
+
+
+def k_scan(heads, flag, mine, ahead, got, ahead_out, total):
+    rows = mine.shape[0] - heads
+    merge(heads, flag, ahead, got, ahead_out, ahead_out.at[pl.ds(rows, heads), :])
+    join(heads, flag[0] == 1, mine, got, total)
+
+
+def k_join(resid, keep, got, gain, total, normed):
+    value = resid[...] + (keep[...] + got[...])
+    total[...] = value
+    normed[...] = norm_rows(value, gain[...])
+
+
+def k_place(place, *refs):
+    out = refs[-1]
+    size = refs[0].shape[0]
+    for piece, ref in enumerate(refs[:-1]):
+        out[rows_at(place, piece, size), :] = ref[:, : out.shape[1]].astype(out.dtype)
+
+
+def project(rounded, wz, wx, wbc, wdt, z, x, bc, dt):
     x[...] = mm(rounded, wx[...], NN)
     bc[...] = mm(rounded, wbc[...], NN)
     dt[...] = mm(rounded, wdt[...], NN)
     z[...] = mm(rounded, wz[...], NN)
+
+
+def k_proj_first(hidden, gain, wz, wx, wbc, wdt, z, x, bc, dt, nb):
+    rounded = norm_rows(hidden[...].astype(F32), gain[...]).astype(BF)
+    nb[...] = rounded
+    project(rounded, wz, wx, wbc, wdt, z, x, bc, dt)
+
+
+def k_proj(place, *refs):
+    pieces, (wz, wx, wbc, wdt, z, x, bc, dt, nb) = refs[:-9], refs[-9:]
+    k_place(place, *pieces, nb)
+    project(nb[...], wz, wx, wbc, wdt, z, x, bc, dt)
 
 
 def conv_rows(ext, halo_rows, rows, weights, bias, aux):
@@ -303,9 +430,10 @@
         yp[:, cols] = result
 
 
-def k_gate(yp, ubc, cum, aux, z, inc, mixed, gated, ss):
+def k_gate(flag, yp, ubc, cum, aux, z, near, far, mixed, gated, ss, inc):
     inner = yp.shape[1]
     heads = cum.shape[1]
+    merge(heads, flag, near, far, inc)
     width = ubc.shape[1] // 2
     emap = head_map(heads, inner)
     c_mat = silu(ubc[:, width:])
@@ -317,22 +445,47 @@
     ss[...] = row_sums(gate * gate)
 
 
-def k_out(layer, total, gated, ss, gain, wout, gn, part):
+def to_relative(place, source, target):
+    pieces = place.shape[0]
+    size = source.shape[0] // pieces
+    for piece in range(pieces):
+        target[piece * size : (piece + 1) * size, :] = source[rows_at(place, piece, size), :]
+
+
+def k_out(layer, total, place, gated, ss, gain, wout, gn, keep, send, moved):
     scale = to_column(lax.rsqrt(ss[...] * (1.0 / total) + eps))
     normed = (gated[...] * scale * gain[layer : layer + 1, :]).astype(BF)
     gn[...] = normed
-    part[...] = mm(normed, wout[...], NN)
-
-
-def k_b1(layer, total, cot, wout, gated, ss, gain, cb, dgn, cross, ggain):
-    rounded = cot[...].astype(BF)
-    cb[...] = rounded
-    grad = mm(rounded, wout[...], NT)
+    to_relative(place, gn, moved)
+    half = keep.shape[0]
+    part = mm(moved[...], wout[...], NN)
+    keep[...] = part[:half, :]
+    send[...] = part[half:, :]
+
+
+def k_b1_top(layer, total, cot, wout, gated, ss, gain, cb, dgn, cross, ggain):
+    cb[...] = cot[...].astype(BF)
+    back_out(layer, total, wout, gated, ss, gain, cb, dgn, ggain)
+    scale_row = lax.rsqrt(ss[...] * (1.0 / total) + eps)
+    cross[...] = scale_row * row_sums(dgn[...] * gated[...] * gain[layer : layer + 1, :])
+
+
+def k_b1(layer, total, place, *refs):
+    pieces, (wout, gated, ss, gain, cb, dgn, cross, ggain) = refs[:-8], refs[-8:]
+    model = cb.shape[1]
+    size = pieces[0].shape[0]
+    for piece, ref in enumerate(pieces):
+        rows = rows_at(place, piece, size)
+        cb[rows, :] = ref[:, :model].astype(BF)
+        cross[rows, :] = ref[:, model : model + 1]
+    back_out(layer, total, wout, gated, ss, gain, cb, dgn, ggain)
+
+
+def back_out(layer, total, wout, gated, ss, gain, cb, dgn, ggain):
+    grad = mm(cb[...], wout[...], NT)
     dgn[...] = grad
     scale = to_column(lax.rsqrt(ss[...] * (1.0 / total) + eps))
-    both = grad * gated[...]
-    cross[...] = row_sums(both * gain[layer : layer + 1, :])
-    ggain[...] = jnp.sum(both * scale, axis=0, keepdims=True)
+    ggain[...] = jnp.sum(grad * gated[...] * scale, axis=0, keepdims=True)
 
 
 def k_b2(layer, total, dgn, gated, mixed, z, ss, cross, gain, ubc, cum, cumt, aux, dm, dz, msg):
@@ -342,7 +495,8 @@
     emap = head_map(heads, inner)
     scale_row = lax.rsqrt(ss[...] * (1.0 / total) + eps)
     scale = to_column(scale_row)
-    pull = to_column(scale_row * scale_row * scale_row * cross[...] * (1.0 / total))
+    dot = to_column(cross[...]) if cross.shape[0] == 1 else cross[...]
+    pull = scale * scale * dot * (1.0 / total)
     d_gated = scale * gain[layer : layer + 1, :] * dgn[...] - gated[...] * pull
     zv = z[...]
     grad = d_gated * silu(zv)
@@ -408,11 +562,12 @@
     gskip[...] = jnp.sum(skip_dot, axis=0, keepdims=True)
 
 
-def k_b4(layer, ux, ubc, dts, dtp, cum, aux, dx, dbc, dcum, ddt, df, inc, dtb, alog,
-         du, dbo, dd, gdtb, galog):
+def k_b4(layer, flag, ux, ubc, dts, dtp, cum, aux, dx, dbc, dcum, ddt, near, far, inc, dtb, alog,
+         du, dbo, dd, gdtb, galog, edge, df):
     rows, inner = ux.shape
     heads = dts.shape[1]
     width = ubc.shape[1] // 2
+    merge(heads, flag, near, far, df)
     emap = head_map(heads, inner)
     conv = ux[...]
     x_conv = silu(conv)
@@ -425,8 +580,11 @@
     to_end_e = expand(to_end, emap)
     dot = per_head(x_conv * spread, emap)
     du[...] = (dx[...] + to_end_e * spread) * silu_slope(conv)
-    dbo[:, :width] = dbc[:, :width] + mm3(x_conv * to_end_e, fin, NN)
-    dbo[:, width:] = dbc[:, width:]
+    slope = silu_slope(ubc[...])
+    dbo[:, :width] = (dbc[:, :width] + mm3(x_conv * to_end_e, fin, NN)) * slope[:, :width]
+    dbo[:, width:] = dbc[:, width:] * slope[:, width:]
+    edge[:, :inner] = du[0:HALO, :]
+    edge[:, inner:] = dbo[0:HALO, :]
     used = to_end * dot
     d_cum = dcum[...] - used
     through = per_head(row_sums(fin * inc[...]) + jnp.zeros((8, inner), F32), emap)[0:1, :]
@@ -444,13 +602,29 @@
 
 def k_conv_back(du, halo, proj, edge, aux, weights, grad, gw, gb, ext_d, ext_p):
     rows = du.shape[0]
-    taps = weights.shape[0]
     ext_d[0:rows, :] = du[...]
     ext_d[rows:, :] = halo[...]
+    conv_back(proj, edge, aux, weights, grad, gw, gb, ext_d, ext_p)
+
+
+def k_conv_back_b(which, du, proj, edge, aux, weights, grad, gw, gb, part, ext_d, ext_p):
+    quarter = du.shape[1]
+    for slot in range(ext_d.shape[1] // quarter):
+        cols = slice(slot * quarter, (slot + 1) * quarter)
+        ext_d[:, cols] = jnp.where(which[0] == slot, du[...], 0.0)
+    wide = conv_back(proj, edge, aux, weights, grad, gw, gb, ext_d, ext_p)
+    part[...] = sum(
+        wide[:, slot * quarter : (slot + 1) * quarter] for slot in range(ext_d.shape[1] // quarter)
+    ).astype(BF)
+
+
+def conv_back(proj, edge, aux, weights, grad, gw, gb, ext_d, ext_p):
+    rows = proj.shape[0]
+    taps = weights.shape[0]
     ext_p[0:HALO, :] = edge[...]
     ext_p[HALO:, :] = proj[...]
     masks = aux[...]
-    value = du[...]
+    value = ext_d[0:rows, :]
     total = jnp.zeros_like(value)
     for tap in range(taps):
         back = ext_d[pl.ds(taps - 1 - tap, rows), :] * weights[tap : tap + 1, :]
@@ -462,23 +636,65 @@
         gw[tap : tap + 1, :] = jnp.sum(seen, axis=0, keepdims=True)
     gb[...] = jnp.sum(value, axis=0, keepdims=True)
     grad[...] = total.astype(BF)
-
-
-def k_dnorm(dz, dxb, dd, dbq, wz, wx, wdt, wbq, own):
+    return total
+
+
+def k_dnorm(place, dz, dxb, dd, dbq, wz, wx, wdt, wbq, keep, send, own, moved):
     own[...] = (
         mm(dz[...], wz[...], NT)
         + mm(dxb[...], wx[...], NT)
         + mm(dd[...], wdt[...], NT)
         + mm(dbq[...], wbq[...], NT)
     )
-
-
-def k_round(value, out):
-    out[...] = value[...].astype(BF)
-
-
-def in_norm(resid, gain_row):
-    return resid * lax.rsqrt(jnp.mean(resid * resid, axis=1) + eps)[:, None] * gain_row[None, :]
+    to_relative(place, own, moved)
+    half = keep.shape[0]
+    keep[...] = moved[0:half, :]
+    send[...] = moved[half:, :]
+
+
+def k_norm_back(resid, keep, got, gain, cot, branch, packed, g_gain):
+    grad = keep[...] + got[...]
+    value = resid[...]
+    inv = lax.rsqrt(jnp.mean(value * value, axis=1, keepdims=True) + eps)
+    unit = value * inv
+    g_gain[...] = jnp.sum(grad * unit, axis=0, keepdims=True)
+    scaled = grad * gain[...]
+    mean = jnp.mean(scaled * unit, axis=1, keepdims=True)
+    total = cot[...] + inv * (scaled - unit * mean)
+    model = value.shape[1]
+    packed[:, :model] = total
+    if branch is not None:
+        rounded = total.astype(BF).astype(F32)
+        dot = jnp.sum(rounded * branch[...], axis=1, keepdims=True)
+        packed[:, model:] = jnp.broadcast_to(dot, (value.shape[0], packed.shape[1] - model))
+
+
+def drop_branch(body, *refs):
+    body(*refs[:5], None, *refs[5:])
+
+
+def k_dw(place, left, *refs):
+    rights, (keep, send, moved, full) = refs[:-4], refs[-4:]
+    pieces = place.shape[0]
+    size = left.shape[1] // pieces
+    half = keep.shape[0]
+    aligned = size % 128 == 0
+    if aligned:
+        for piece in range(pieces):
+            moved[:, piece * size : (piece + 1) * size] = left[:, rows_at(place, piece, size)]
+    start = 0
+    for right in rights:
+        cols = slice(start, start + right.shape[1])
+        start += right.shape[1]
+        if aligned:
+            keep[:, cols] = mm(moved[:, :half], right[...], TN)
+            send[:, cols] = mm(moved[:, half:], right[...], TN)
+        else:
+            full[:, cols] = mm(left[...], right[...], TN)
+    if not aligned:
+        for piece in range(pieces):
+            target, row = (keep, piece) if piece < pieces // 2 else (send, piece - pieces // 2)
+            target[row * size : (row + 1) * size, :] = full[rows_at(place, piece, size), :]
 
 
 def local(hidden_in, seg_ids, norm_gain, w_z, w_x, w_bc, w_dt, conv_x_w, conv_x_b, conv_bc_w,
@@ -492,8 +708,21 @@
     taps = conv_x_w.shape[1]
     inner_total = inner * lax.axis_size("head")
     seq_bits = bits_of("seq")
-    top_down = list(reversed(range(1, seq_bits)))
-    orders = ([0] + top_down, top_down + [0], top_down[:1] + [0] + top_down[1:])
+    spare = list(range(3, seq_bits))
+    orders = [
+        [bit for bit in base if bit < seq_bits] + spare
+        for base in ([0, 1, 2], [1, 2, 0], [2, 0, 1])
+    ]
+    share = model // lax.axis_size("seq")
+    places = [seq_places(order, share) for order in orders]
+    head_bits = bits_of("head")
+    size = rows // lax.axis_size("head")
+    place = jnp.stack(
+        [
+            reverse_bits(lax.axis_index("head") ^ mask, head_bits) * size
+            for mask in relative_order(head_bits)
+        ]
+    ).astype(jnp.int32)
 
     padded = jnp.concatenate(
         [jnp.full((taps - 1,), -1, jnp.int32), seg_ids, jnp.full((taps - 1,), -1, jnp.int32)]
@@ -509,163 +738,240 @@
     aux = jnp.stack(columns, axis=1).astype(F32)
     segc, segr = own[:, None], own[None, :]
 
-    resid = own_piece(hidden_in.astype(F32), "head", 0)
+    own_quarter = reverse_bits(lax.axis_index("head"), head_bits).reshape(1).astype(jnp.int32)
+    half_rows = ((rows // 2, model), F32)
+    quarter_rows = ((size, model), F32)
+    proj_outs = [((rows, inner), F32), ((rows, inner), F32), ((rows, state2), F32),
+                 ((rows, heads), F32), ((rows, model), BF)]
+    message = ((inner + heads, width), F32)
+
+    resid = own_piece(hidden_in, "head", 0).astype(F32)
+    normed = None
     saved = []
     for l in range(layers):
+        weights = (Far(w_z, l), Far(w_x, l), Far(w_bc, l), Far(w_dt, l))
         if l == 0:
-            normed_f = in_norm(hidden_in.astype(F32), norm_gain[l])
+            z, x, bc, dtp, nb = run(
+                k_proj_first, proj_outs, hidden_in, norm_gain[l : l + 1], *weights, name="proj"
+            )
         else:
-            normed_f = gather_back(in_norm(resid, norm_gain[l]), "head", 0)
-        z, x, bc, dtp, nb = run(
-            k_proj,
-            [((rows, inner), F32), ((rows, inner), F32), ((rows, state2), F32),
-             ((rows, heads), F32), ((rows, model), BF)],
-            normed_f, w_z, w_x, w_bc, w_dt, blocks={1: l, 2: l, 3: l, 4: l}, name="proj",
-        )
+            z, x, bc, dtp, nb = run(
+                k_proj, proj_outs, *gather_pieces(normed, "head"), *weights, small=[place],
+                name="proj",
+            )
         edge = rotate(jnp.concatenate([x[rows - HALO :], bc[rows - HALO :]], 1), "seq", 1)
         ux, ubc, dts, cum, cumt, msg = run(
             functools.partial(k_front, l),
             [((rows, inner), F32), ((rows, state2), F32), ((rows, heads), F32),
-             ((rows, heads), F32), ((heads, rows), F32), ((inner + heads, width), F32)],
-            x, bc, dtp, edge, aux, conv_x_w, conv_x_b, conv_bc_w, conv_bc_b, dt_bias, a_log,
-            blocks={5: l, 7: l},
+             ((rows, heads), F32), ((heads, rows), F32), message],
+            x, bc, dtp, edge, aux, conv_x_w[l], conv_x_b, conv_bc_w[l], conv_bc_b, dt_bias, a_log,
             scratch=(pltpu.VMEM((rows + HALO, inner), F32), pltpu.VMEM((rows + HALO, state2), F32)),
             name="front",
         )
-        inc = carried(msg, heads, False)
+        near, far, flag = carried(msg, heads, False)
         (yp,) = run(
             functools.partial(k_intra, l), [((rows, inner), F32)],
             ux, ubc, dts, cum, cumt, segc, segr, d_skip, name="intra",
         )
-        mixed, gated, ss = run(
-            k_gate, [((rows, inner), F32), ((rows, inner), F32), ((1, rows), F32)],
-            yp, ubc, cum, aux, z, inc, name="gate",
+        mixed, gated, ss, inc = run(
+            k_gate,
+            [((rows, inner), F32), ((rows, inner), F32), ((1, rows), F32), ((inner, width), F32)],
+            yp, ubc, cum, aux, z, near, far, small=[flag], name="gate",
         )
         ss = lax.psum(ss, "head")
-        gn, part = run(
+        gn, keep, send = run(
             functools.partial(k_out, l, inner_total),
-            [((rows, inner), BF), ((rows, model), F32)],
-            gated, ss, gate_gain, w_out, blocks={3: l}, name="out",
-        )
-        branch = scatter_sum(part, "head", 0)
+            [((rows, inner), BF), half_rows, half_rows],
+            gated, ss, gate_gain, Far(w_out, l), small=[place],
+            scratch=(pltpu.VMEM((rows, inner), BF),), name="out",
+        )
+        keep, got = finish_scatter(keep, send, "head")
         saved.append((resid, z, x, bc, dtp, nb, edge, ux, ubc, dts, cum, cumt, inc, mixed, gated,
-                      ss, gn))
-        resid = resid + branch
+                      ss, gn, keep + got))
+        last = l + 1 == layers
+        resid, normed = run(
+            k_join, [quarter_rows, quarter_rows], resid, keep, got,
+            norm_gain[0 if last else l + 1][None, :], flops=1000000, name="join",
+        )
     (hidden_out,) = run(
-        k_round, [((rows, model), BF)], gather_back(resid, "head", 0), flops=1000000, name="round"
+        k_place, [((rows, model), BF)], *gather_pieces(resid, "head"), small=[place],
+        flops=1000000, name="round",
     )
 
-    cot_full = out_cot
+    def dw_scratch(cols):
+        aligned = share % 128 == 0
+        return (
+            pltpu.VMEM((rows, model if aligned else 128), BF),
+            pltpu.VMEM((8 if aligned else model, cols), F32),
+        )
+
     cot = own_piece(out_cot, "head", 0)
-    wide = [[None] * layers for _ in range(3)]
-    narrow = [None] * layers
+    packed = None
+    final = [[None] * layers for _ in range(3)]
+    narrow_in = [None] * layers
     small = [None] * layers
     gains = [None] * layers
+    waiting = []
+    block = (model // 2, inner)
     for l in reversed(range(layers)):
-        (resid, z, x, bc, dtp, nb, edge, ux, ubc, dts, cum, cumt, inc, mixed, gated, ss,
-         gn) = saved[l]
-        cb, dgn, cross, ggain = run(
-            functools.partial(k_b1, l, inner_total),
-            [((rows, model), BF), ((rows, inner), F32), ((1, rows), F32), ((1, inner), F32)],
-            cot_full, w_out, gated, ss, gate_gain, blocks={1: l}, name="b1",
-        )
-        cross = lax.psum(cross, "head")
+        (resid, z, x, bc, dtp, nb, edge, ux, ubc, dts, cum, cumt, inc, mixed, gated, ss, gn,
+         branch) = saved[l]
+        b1_outs = [((rows, model), BF), ((rows, inner), F32)]
+        if packed is None:
+            cb, dgn, cross, ggain = run(
+                functools.partial(k_b1_top, l, inner_total),
+                b1_outs + [((1, rows), F32), ((1, inner), F32)],
+                out_cot, Far(w_out, l), Far(gated), ss, gate_gain, name="b1",
+            )
+            cross = lax.psum(cross, "head")
+        else:
+            cb, dgn, cross, ggain = run(
+                functools.partial(k_b1, l, inner_total),
+                b1_outs + [((rows, 1), F32), ((1, inner), F32)],
+                *gather_pieces(packed, "head"), Far(w_out, l), Far(gated), ss, gate_gain, small=[place],
+                name="b1",
+            )
         dm, dz, msg = run(
             functools.partial(k_b2, l, inner_total),
-            [((rows, inner), F32), ((rows, inner), BF), ((inner + heads, width), F32)],
-            dgn, gated, mixed, z, ss, cross, gate_gain, ubc, cum, cumt, aux, name="b2",
-        )
-        fin = carried(msg, heads, True)
+            [((rows, inner), F32), ((rows, inner), BF), message],
+            dgn, Far(gated), Far(mixed), Far(z), ss, cross, gate_gain, Far(ubc), Far(cum), Far(cumt), aux,
+            after=waiting,
+            name="b2",
+        )
+        near, far, flag = carried(msg, heads, True)
         dx, dbc, dcum, ddt, gskip = run(
             functools.partial(k_b3, l),
             [((rows, inner), F32), ((rows, state2), F32), ((rows, heads), F32),
              ((rows, heads), F32), ((1, heads), F32)],
-            dm, ux, ubc, dts, cum, cumt, segc, segr, mixed, inc, aux, d_skip, name="b3",
-        )
-        du, dbo, dd, gdtb, galog = run(
+            dm, Far(ux), Far(ubc), Far(dts), Far(cum), Far(cumt), segc, segr, Far(mixed), Far(inc), aux,
+            d_skip, name="b3",
+        )
+        du, dub, dd, gdtb, galog, first_rows = run(
             functools.partial(k_b4, l),
             [((rows, inner), F32), ((rows, state2), F32), ((rows, heads), BF),
-             ((1, heads), F32), ((1, heads), F32)],
-            ux, ubc, dts, dtp, cum, aux, dx, dbc, dcum, ddt, fin, inc, dt_bias, a_log, name="b4",
-        )
-        halo_x = rotate(du[:HALO], "seq", -1)
-        dbq = scatter_sum(dbo, "head", 1)
-        dub = dbq * silu_slope(own_piece(ubc, "head", 1))
-        halo_b = rotate(dub[:HALO], "seq", -1)
+             ((1, heads), F32), ((1, heads), F32), ((HALO, inner + state2), F32)],
+            Far(ux), Far(ubc), Far(dts), Far(dtp), Far(cum), aux, dx, dbc, dcum, ddt, near, far,
+            Far(inc), dt_bias, a_log,
+            small=[flag], scratch=(pltpu.VMEM((inner, width), F32),), name="b4",
+        )
+        halo = rotate(first_rows, "seq", -1)
+        dub = scatter_cols(jnp.concatenate([dub, halo[:, inner:]], 0), "head")
         quarter = dub.shape[1]
         dxb, gcw, gcb = run(
             k_conv_back,
             [((rows, inner), BF), ((taps, inner), F32), ((1, inner), F32)],
-            du, halo_x, x, edge[:, :inner], aux, conv_x_w, blocks={5: l},
+            du, halo[:, :inner], Far(x), edge[:, :inner], aux, conv_x_w[l],
             scratch=(pltpu.VMEM((rows + HALO, inner), F32), pltpu.VMEM((rows + HALO, inner), F32)),
             name="convx",
         )
-        dbb, gbw, gbb = run(
-            k_conv_back,
-            [((rows, quarter), BF), ((taps, quarter), F32), ((1, quarter), F32)],
-            dub, halo_b, own_piece(bc, "head", 1), own_piece(edge[:, inner:], "head", 1), aux,
-            own_piece(conv_bc_w[l], "head", 1),
-            scratch=(pltpu.VMEM((rows + HALO, quarter), F32),
-                     pltpu.VMEM((rows + HALO, quarter), F32)),
+        dbw, gbw, gbb, dbb = run(
+            k_conv_back_b,
+            [((rows, state2), BF), ((taps, state2), F32), ((1, state2), F32), ((rows, quarter), BF)],
+            dub, Far(bc), edge[:, inner:], aux, conv_bc_w[l], small=[own_quarter],
+            scratch=(pltpu.VMEM((rows + HALO, state2), F32),
+                     pltpu.VMEM((rows + HALO, state2), F32)),
             name="convb",
         )
-        (part,) = run(
-            k_dnorm, [((rows, model), F32)],
-            dz, dxb, dd, dbb, w_z, w_x, w_dt, own_piece(w_bc[l], "head", 1),
-            blocks={4: l, 5: l, 6: l}, name="dnorm",
-        )
-        d_normed = scatter_sum(part, "head", 0)
-        wide[2][l] = seq_scatter(mm(cb, gn, TN), orders[2])
-        wide[0][l] = seq_scatter(mm(nb, dz, TN), orders[0])
-        wide[1][l] = seq_scatter(mm(nb, dxb, TN), orders[1])
-        narrow[l] = seq_scatter(
-            jnp.concatenate([mm(nb, dbb, TN), mm(nb, dd, TN)], axis=1), orders[0]
-        )
-        _, norm_pull = jax.vjp(in_norm, resid, norm_gain[l])
-        d_resid, d_gain = norm_pull(d_normed)
-        gains[l] = d_gain
+        keep, send = run(
+            k_dnorm, [half_rows, half_rows],
+            dz, dxb, dd, dbw, Far(w_z, l), Far(w_x, l), Far(w_dt, l), Far(w_bc, l), small=[place],
+            scratch=(pltpu.VMEM((rows, model), F32), pltpu.VMEM((rows, model), F32)), name="dnorm",
+        )
+        keep, got = finish_scatter(keep, send, "head")
+        cols = model + 128 if l > 0 else model
+        body = k_norm_back if l > 0 else functools.partial(drop_branch, k_norm_back)
+        cot_args = (resid, keep, got, norm_gain[l : l + 1], cot)
+        packed, gains[l] = run(
+            body, [((size, cols), F32), ((1, model), F32)],
+            *(cot_args + ((saved[l - 1][-1],) if l > 0 else ())), flops=1000000, name="normback",
+        )
+        cot = packed[:, :model]
+
+        def product(slot, left, right, after):
+            return run(
+                k_dw, [(block, F32), (block, F32)], left, right, small=[places[slot]],
+                after=after, scratch=dw_scratch(inner), name="dw",
+            )
+
+        steps = [
+            product(2, cb, Far(gn), [halo]),
+            product(0, Far(nb), dz, [halo]),
+            product(1, Far(nb), dxb, []),
+        ]
+        slots = (2, 0, 1)
+        waiting = []
+        for slot, (keep, send) in zip(slots, steps):
+            for index, bit in enumerate(orders[slot]):
+                ended = index + 1 == seq_bits
+                keep, send = seq_step(keep, send, bit, ended)
+            final[slot][l] = keep
+            if slot != 1:
+                waiting.append(keep)
+        narrow_in[l] = (Far(nb), dbb, dd)
         small[l] = (gcw, gcb, gbw, gbb, gdtb, galog, gskip, ggain)
-        cot = cot + d_resid
-        cot_full = gather_back(cot, "head", 0)
-
-    flat = [part.reshape(-1) for l in range(layers) for part in small[l]] + gains
-    sizes = [part.size for part in flat]
-    packed = jnp.concatenate(flat)
-    packed = jnp.pad(packed, (0, -packed.size % 1024)).reshape(-1, 128)
-    packed = seq_sum(packed).reshape(-1)
-    pieces, start = [], 0
-    for size in sizes:
-        pieces.append(packed[start : start + size])
-        start += size
+    (grad_in,) = run(
+        k_place, [((rows, model), F32)], *gather_pieces(cot, "head"), small=[place],
+        flops=1000000, name="place",
+    )
+
+    narrow = [
+        run(
+            k_dw, [((model // 2, quarter + heads), F32)] * 2, *narrow_in[l], small=[places[0]],
+            scratch=dw_scratch(quarter + heads), name="dwn",
+        )
+        for l in range(layers)
+    ]
+    keep = jnp.concatenate([pair[0] for pair in narrow], 1)
+    send = jnp.concatenate([pair[1] for pair in narrow], 1)
+    for index, bit in enumerate(orders[0]):
+        keep, send = seq_step(keep, send, bit, index + 1 == seq_bits)
+    narrow = jnp.stack(jnp.split(keep, layers, 1))
+
+    def reduced(flat, order):
+        sizes = [part.size for part in flat]
+        pack = jnp.concatenate([part.reshape(-1) for part in flat])
+        pack = jnp.pad(pack, (0, -pack.size % 1024)).reshape(-1, 128)
+        pack = seq_sum(pack, order).reshape(-1)
+        pieces, start = [], 0
+        for count in sizes:
+            pieces.append(pack[start : start + count])
+            start += count
+        return pieces
+
+    pieces = reduced([part for l in range(layers) for part in small[l]], orders[1])
     count = len(small[0])
 
     def both(slot):
         return jnp.stack([pieces[l * count + slot].reshape(small[l][slot].shape) for l in range(layers)])
 
-    grad_gain = head_sum(jnp.stack(pieces[layers * count :]))
-    share = model // lax.axis_size("seq")
+    wide = jnp.concatenate(
+        [seq_sum(jnp.concatenate(gains, 0), orders[2]).reshape(-1), both(2).reshape(-1),
+         both(3).reshape(-1)]
+    )
+    wide = head_sum(wide.reshape(-1, 128)).reshape(-1)
+    stop = layers * model
+    grad_gain = wide[:stop].reshape(layers, model)
     grad_gain = lax.dynamic_slice_in_dim(grad_gain, lax.axis_index("seq") * share, share, 1)
-    quarter = state2 // lax.axis_size("head")
-    narrow = jnp.stack(narrow)
-    bc_parts = jnp.concatenate([narrow[:, :, :quarter], both(2), both(3)], axis=1)
-    bc_parts = gather_back(bc_parts, "head", 2)
+    bc_w = wide[stop : stop + layers * taps * state2].reshape(layers, taps, state2)
+    bc_b = wide[stop + layers * taps * state2 :].reshape(layers, state2)
+    bc_parts = gather_back(narrow[:, :, :quarter], "head", 2)
     return (
         hidden_out,
-        cot_full,
+        grad_in,
         grad_gain,
-        jnp.stack(wide[0]),
-        jnp.stack(wide[1]),
-        bc_parts[:, :share],
+        jnp.stack(final[0]),
+        jnp.stack(final[1]),
+        bc_parts,
         narrow[:, :, quarter:],
         both(0),
         both(1)[:, 0],
-        bc_parts[:, share : share + taps],
-        bc_parts[:, share + taps],
+        bc_w,
+        bc_b,
         both(4)[:, 0],
         both(5)[:, 0],
         both(6)[:, 0],
         both(7)[:, 0],
-        jnp.stack([part.T for part in wide[2]]),
+        jnp.stack([part.T for part in final[2]]),
     )
 
 

time: 616 us -> 503 us (0.82)
  starting transfers between devices: 210 us -> 99.9 us
  waiting for transfers between devices: 139 us -> 207 us
  other arithmetic: 66.5 us -> 16.8 us
  Pallas kernels: 89.3 us -> 73.5 us
  local copies, waits for them, and re-layouts: 62.9 us -> 74.6 us
  matrix products: 9.33 us -> 0 us
  blocking collectives: 27.2 us -> 18.3 us
    ppermute x63 -> x67, starting transfers between devices: 192 us -> 91.7 us  [swap(): return lax.ppermute(value, axis, [(i, i ^ mask) for i in range(count)])]
    ppermute x63 -> x67, waiting for transfers between devices: 132 us -> 198 us  [swap(): return lax.ppermute(value, axis, [(i, i ^ mask) for i in range(count)])]
    unnamed x158 -> x403, local copies, waits for them, and re-layouts: 20.2 us -> 65.3 us
    dynamic_slice x35 -> x3, local copies, waits for them, and re-layouts: 21.2 us -> 0.76 us  [the longest x1 0.56 us: local(): lax.dynamic_slice_in_dim(grad_gain, lax.axis_index('seq') * share, share, 1)]
    add x26 -> x12, other arithmetic: 20.5 us -> 4.19 us  [the longest x4 2.87 us: finish_scatter(): send = keep[half:] + got[half:]]
    pallas_call x25 -> x60, Pallas kernels: 89.3 us -> 73.5 us  [run(): pl.pallas_call(inner, in_specs=[pl.BlockSpec(memory_space=pltpu.SMEM)] *...]
    select_n x16 -> x0, other arithmetic: 10.6 us -> none  [the longest x4 5.02 us: carried(): jnp.where(later, ahead_d * got_s + ahead_s, ahead_s)]
    ppermute x6 -> x4, starting transfers between devices: 17.9 us -> 8.17 us  [rotate(): lax.ppermute(value, axis, [(i, (i + steps) % count) for i in range(count)])]
  transfers between devices with their start and end apart: 69 -> 71, of which waited for: 30 -> 38; matrix products, arithmetic and copies ran while one was open for 19% -> 6% of each run, Pallas kernels for 9% -> 11%
where the time goes in v2:
time: 503 us; the launch traced here: 494 us
  waiting for transfers between devices  207 us (41%)
  starting transfers between devices  99.9 us (20%)
  local copies, waits for them, and re-layouts  74.6 us (15%)
  Pallas kernels  73.5 us (15%)
  blocking collectives  18.3 us (4%)
  other arithmetic  16.8 us (3%)
    ppermute x67, waiting for transfers between devices, swap(): return lax.ppermute(value, axis, [(i, i ^ mask) for i in range(count)])  198 us
    ppermute x67, starting transfers between devices, swap(): return lax.ppermute(value, axis, [(i, i ^ mask) for i in range(count)])  91.7 us
    pallas_call x60, Pallas kernels, run(): pl.pallas_call(inner, in_specs=[pl.BlockSpec(memory_space=pltpu.SMEM)] *...  73.5 us
    unnamed x403, local copies, waits for them, and re-layouts  65.3 us
    psum x2, blocking collectives, local(): ss = lax.psum(ss, 'head')  11.3 us
  transfers between devices with their start and end apart: 71, of which 38 were waited for; matrix products, arithmetic and copies ran while one was open for 6% of the time, Pallas kernels for 11%

profile of v2, /device:TPU:0, one launch (start us, length us, event | category | flops | bytes accessed | tf_op | source)
XLA Modules:
  0.0 493.7 jit_solution(15923646691488616478)
XLA Ops:
  21.2 7.2 %collective-permute-done.1.refs_2_ = f32[520,128]{1,0:T(8,128)S(1)} collective-permute-done((f32[520,128]{1,0:T(8,128)S(1)}, f32[520,128]{1,0:T(8,128)S(1)}, u32[]{:S(2)}, u32[]{:S(2)}) %collective-permute-start.1) | collective-permute-done | bytes 266272 | tf_op jit(solution)/shard_map/ppermute | solution.py:19
  28.8 6.2 %collective-permute-done.2.refs_3_ = f32[520,128]{1,0:T(8,128)S(1)} collective-permute-done((f32[520,128]{1,0:T(8,128)S(1)}, f32[520,128]{1,0:T(8,128)S(1)}, u32[]{:S(2)}, u32[]{:S(2)}) %collective-permute-start.2) | collective-permute-done | bytes 266272 | tf_op jit(solution)/shard_map/ppermute | solution.py:19
  45.4 5.6 %psum.21.refs_2_.refs_7_.refs_4_ = f32[1,256]{1,0:T(1,128)S(1)} all-reduce(f32[1,256]{1,0:T(1,128)S(1)} %get-tuple-element.188), channel_id=1, replica_groups=mesh['seq'=8,'head'=4] {'head'}, use_global_device_ids=true, to_apply=%region_0.0 | all-reduce | flops 256 | bytes 2048 | tf_op jit(solution)/shard_map/psum | solution.py:781
  59.6 5.5 %collective-permute-done.5.refs_2_ = f32[64,1024]{1,0:T(8,128)S(1)} collective-permute-done((f32[64,1024]{1,0:T(8,128)S(1)}, f32[64,1024]{1,0:T(8,128)S(1)}, u32[]{:S(2)}, u32[]{:S(2)}) %collective-permute-start.5) | collective-permute-done | bytes 262176 | tf_op jit(solution)/shard_map/ppermute | solution.py:19
  68.1 5.8 %collective-permute-done.6.refs_2_ = f32[64,1024]{1,0:T(8,128)S(1)} collective-permute-done((f32[64,1024]{1,0:T(8,128)S(1)}, f32[64,1024]{1,0:T(8,128)S(1)}, u32[]{:S(2)}, u32[]{:S(2)}) %collective-permute-start.6) | collective-permute-done | bytes 262176 | tf_op jit(solution)/shard_map/ppermute | solution.py:19
  81.6 6.0 %collective-permute-done.9.refs_3_ = f32[8,768]{1,0:T(8,128)S(1)} collective-permute-done((f32[8,768]{1,0:T(8,128)S(1)}, f32[8,768]{1,0:T(8,128)S(1)}, u32[]{:S(2)}, u32[]{:S(2)}) %collective-permute-start.9) | collective-permute-done | bytes 24608 | tf_op jit(solution)/shard_map/ppermute | solution.py:24
  89.7 7.3 %collective-permute-done.10.refs_2_ = f32[520,128]{1,0:T(8,128)S(1)} collective-permute-done((f32[520,128]{1,0:T(8,128)S(1)}, f32[520,128]{1,0:T(8,128)S(1)}, u32[]{:S(2)}, u32[]{:S(2)}) %collective-permute-start.10) | collective-permute-done | bytes 266272 | tf_op jit(solution)/shard_map/ppermute | solution.py:19
  115.5 5.6 %psum.22.refs_2_.refs_3_.refs_4_ = f32[1,256]{1,0:T(1,128)S(1)} all-reduce(f32[1,256]{1,0:T(1,128)S(1)} %get-tuple-element.208), channel_id=1, replica_groups=mesh['seq'=8,'head'=4] {'head'}, use_global_device_ids=true, to_apply=%region_1.0 | all-reduce | flops 256 | bytes 2048 | tf_op jit(solution)/shard_map/psum | solution.py:781
  126.6 7.1 %psum.23.refs_5_ = f32[1,256]{1,0:T(1,128)S(1)} all-reduce(f32[1,256]{1,0:T(1,128)S(1)} %get-tuple-element.214), channel_id=1, replica_groups=mesh['seq'=8,'head'=4] {'head'}, use_global_device_ids=true, to_apply=%region_2.0 | all-reduce | flops 256 | bytes 2048 | tf_op jit(solution)/shard_map/psum | solution.py:826
  141.1 6.0 %collective-permute-done.18.refs_2_ = f32[520,128]{1,0:T(8,128)S(1)} collective-permute-done((f32[520,128]{1,0:T(8,128)S(1)}, f32[520,128]{1,0:T(8,128)S(1)}, u32[]{:S(2)}, u32[]{:S(2)}) %collective-permute-start.18) | collective-permute-done | bytes 266272 | tf_op jit(solution)/shard_map/ppermute | solution.py:19
  147.2 4.9 collective-permute-start.19
  202.1 6.7 %collective-permute-done.29.refs_1_ = f32[512,512]{1,0:T(8,128)S(1)} collective-permute-done((f32[512,512]{1,0:T(8,128)S(1)}, f32[512,512]{1,0:T(8,128)S(1)}, u32[]{:S(2)}, u32[]{:S(2)}) %collective-permute-start.29) | collective-permute-done | bytes 1048608 | tf_op jit(solution)/shard_map/ppermute | solution.py:19
  212.1 21.5 %collective-permute-start.33 = (f32[256,512]{1,0:T(8,128)S(1)}, f32[256,512]{1,0:T(8,128)S(1)}, u32[]{:S(2)}, u32[]{:S(2)}) collective-permute-start(f32[256,512]{1,0:T(8,128)S(1)} %get-tuple-element.251), channel_id=1, source_target_pairs={{0,8},{4,12},{8,0},{12,4},{16,24},{20,28},{24,16},{28,20},{1,9},{5... | collective-permute-start | bytes 1572872 | tf_op jit(solution)/shard_map/ppermute | solution.py:19
  237.4 6.7 %collective-permute-done.26.refs_2_ = f32[64,1152]{1,0:T(8,128)S(1)} collective-permute-done((f32[64,1152]{1,0:T(8,128)S(1)}, f32[64,1152]{1,0:T(8,128)S(1)}, u32[]{:S(2)}, u32[]{:S(2)}) %collective-permute-start.26) | collective-permute-done | bytes 294944 | tf_op jit(solution)/shard_map/ppermute | solution.py:19
  253.2 21.0 %collective-permute-done.31 = f32[128,512]{1,0:T(8,128)S(1)} collective-permute-done((f32[128,512]{1,0:T(8,128)S(1)}, f32[128,512]{1,0:T(8,128)S(1)}, u32[]{:S(2)}, u32[]{:S(2)}) %collective-permute-start.31) | collective-permute-done | bytes 262176 | tf_op jit(solution)/shard_map/ppermute | solution.py:19
  274.3 6.6 %collective-permute-done.34 = f32[128,512]{1,0:T(8,128)S(1)} collective-permute-done((f32[128,512]{1,0:T(8,128)S(1)}, f32[128,512]{1,0:T(8,128)S(1)}, u32[]{:S(2)}, u32[]{:S(2)}) %collective-permute-start.34) | collective-permute-done | bytes 262176 | tf_op jit(solution)/shard_map/ppermute | solution.py:19
  294.7 12.4 %collective-permute-done.36.refs_3_ = f32[520,128]{1,0:T(8,128)S(1)} collective-permute-done((f32[520,128]{1,0:T(8,128)S(1)}, f32[520,128]{1,0:T(8,128)S(1)}, u32[]{:S(2)}, u32[]{:S(2)}) %collective-permute-start.36) | collective-permute-done | bytes 266272 | tf_op jit(solution)/shard_map/ppermute | solution.py:19
  320.4 4.8 b3.3
  365.5 21.7 %collective-permute-done.49 = f32[72,128]{1,0:T(8,128)S(1)} collective-permute-done((f32[72,128]{1,0:T(8,128)S(1)}, f32[72,128]{1,0:T(8,128)S(1)}, u32[]{:S(2)}, u32[]{:S(2)}) %collective-permute-start.49) | collective-permute-done | bytes 36896 | tf_op jit(solution)/shard_map/ppermute | solution.py:19
  394.9 11.3 %collective-permute-done.51 = f32[72,128]{1,0:T(8,128)S(1)} collective-permute-done((f32[72,128]{1,0:T(8,128)S(1)}, f32[72,128]{1,0:T(8,128)S(1)}, u32[]{:S(2)}, u32[]{:S(2)}) %collective-permute-start.51) | collective-permute-done | bytes 36896 | tf_op jit(solution)/shard_map/ppermute | solution.py:19
  423.4 5.3 %collective-permute-done.65 = f32[128,144]{1,0:T(8,128)S(1)} collective-permute-done((f32[128,144]{1,0:T(8,128)S(1)}, f32[128,144]{1,0:T(8,128)S(1)}, u32[]{:S(2)}, u32[]{:S(2)}) %collective-permute-start.65) | collective-permute-done | bytes 73760 | tf_op jit(solution)/shard_map/ppermute | solution.py:19
  431.3 4.9 collective-permute-done.46
  470.9 10.1 %collective-permute-done.58.refs_1_ = f32[256,512]{1,0:T(8,128)S(1)} collective-permute-done((f32[256,512]{1,0:T(8,128)}, f32[256,512]{1,0:T(8,128)S(1)}, u32[]{:S(2)}, u32[]{:S(2)}) %collective-permute-start.58) | collective-permute-done | bytes 524320 | tf_op jit(solution)/shard_map/ppermute | solution.py:19
  481.4 5.0 %collective-permute-done.70 = f32[128,512]{1,0:T(8,128)} collective-permute-done((f32[128,512]{1,0:T(8,128)}, f32[128,512]{1,0:T(8,128)}, u32[]{:S(2)}, u32[]{:S(2)}) %collective-permute-start.70) | collective-permute-done | bytes 262176 | tf_op jit(solution)/shard_map/ppermute | solution.py:19
  (693 shorter events, 285.3 us)
Async XLA Ops:
  181.3 27.5 %collective-permute-start.29 = (f32[512,512]{1,0:T(8,128)S(1)}, f32[512,512]{1,0:T(8,128)S(1)}, u32[]{:S(2)}, u32[]{:S(2)}) collective-permute-start(f32[512,512]{1,0:T(8,128)S(1)} %get-tuple-element.242), channel_id=1, source_target_pairs={{0,24},{4,28},{8,16},{12,20},{16,8},{20,12},{24,0},{28,4},{1,25},{... | collective-permute-start | bytes 3145736 | tf_op jit(solution)/shard_map/ppermute | solution.py:19
  184.3 27.6 %collective-permute-start.32 = (f32[512,512]{1,0:T(8,128)}, f32[512,512]{1,0:T(8,128)S(1)}, u32[]{:S(2)}, u32[]{:S(2)}) collective-permute-start(f32[512,512]{1,0:T(8,128)} %get-tuple-element.249), channel_id=1, source_target_pairs={{0,4},{4,0},{8,12},{12,8},{16,20},{20,16},{24,28},{28,24},{1,5},{5... | collective-permute-start | bytes 3145736 | tf_op jit(solution)/shard_map/ppermute | solution.py:19
  200.9 33.6 %collective-permute-start.25 = (f32[64,1024]{1,0:T(8,128)}, f32[64,1024]{1,0:T(8,128)S(1)}, u32[]{:S(2)}, u32[]{:S(2)}) collective-permute-start(f32[64,1024]{1,0:T(8,128)} %get-tuple-element.382), channel_id=1, source_target_pairs={{0,2},{1,3},{2,0},{3,1},{4,6},{5,7},{6,4},{7,5},{8,10},{9,11},{10,... | collective-permute-start | bytes 786440 | tf_op jit(solution)/shard_map/ppermute | solution.py:19
  210.6 33.5 %collective-permute-start.30 = (f32[256,512]{1,0:T(8,128)}, f32[256,512]{1,0:T(8,128)}, u32[]{:S(2)}, u32[]{:S(2)}) collective-permute-start(f32[256,512]{1,0:T(8,128)} %get-tuple-element.244), channel_id=1, source_target_pairs={{0,4},{4,0},{8,12},{12,8},{16,20},{20,16},{24,28},{28,24},{1,5},{5... | collective-permute-start | bytes 1572872 | tf_op jit(solution)/shard_map/ppermute | solution.py:19
  211.9 36.6 %collective-permute-start.13 = (f32[128,1024]{1,0:T(8,128)}, f32[128,1024]{1,0:T(8,128)S(1)}, u32[]{:S(2)}, u32[]{:S(2)}) collective-permute-start(f32[128,1024]{1,0:T(8,128)} %copy-done.90), channel_id=1, source_target_pairs={{0,1},{1,0},{2,3},{3,2},{4,5},{5,4},{6,7},{7,6},{8,9},{9,8},{10,11... | collective-permute-start | bytes 1572872 | tf_op jit(solution)/shard_map/ppermute | solution.py:19
  212.1 34.3 %collective-permute-start.33 = (f32[256,512]{1,0:T(8,128)S(1)}, f32[256,512]{1,0:T(8,128)S(1)}, u32[]{:S(2)}, u32[]{:S(2)}) collective-permute-start(f32[256,512]{1,0:T(8,128)S(1)} %get-tuple-element.251), channel_id=1, source_target_pairs={{0,8},{4,12},{8,0},{12,4},{16,24},{20,28},{24,16},{28,20},{1,9},{5... | collective-permute-start | bytes 1572872 | tf_op jit(solution)/shard_map/ppermute | solution.py:19
  237.3 48.2 %collective-permute-start.60 = (f32[512,512]{1,0:T(8,128)S(1)}, f32[512,512]{1,0:T(8,128)S(1)}, u32[]{:S(2)}, u32[]{:S(2)}) collective-permute-start(f32[512,512]{1,0:T(8,128)S(1)} %get-tuple-element.307), channel_id=1, source_target_pairs={{0,8},{4,12},{8,0},{12,4},{16,24},{20,28},{24,16},{28,20},{1,9},{5... | collective-permute-start | bytes 3145736 | tf_op jit(solution)/shard_map/ppermute | solution.py:19
  246.3 27.9 %collective-permute-start.31 = (f32[128,512]{1,0:T(8,128)S(1)}, f32[128,512]{1,0:T(8,128)S(1)}, u32[]{:S(2)}, u32[]{:S(2)}) collective-permute-start(f32[128,512]{1,0:T(8,128)S(1)} %get-tuple-element.246), channel_id=1, source_target_pairs={{0,8},{4,12},{8,0},{12,4},{16,24},{20,28},{24,16},{28,20},{1,9},{5... | collective-permute-start | bytes 786440 | tf_op jit(solution)/shard_map/ppermute | solution.py:19
  248.4 32.4 %collective-permute-start.34 = (f32[128,512]{1,0:T(8,128)S(1)}, f32[128,512]{1,0:T(8,128)S(1)}, u32[]{:S(2)}, u32[]{:S(2)}) collective-permute-start(f32[128,512]{1,0:T(8,128)S(1)} %get-tuple-element.253), channel_id=1, source_target_pairs={{0,24},{4,28},{8,16},{12,20},{16,8},{20,12},{24,0},{28,4},{1,25},{... | collective-permute-start | bytes 786440 | tf_op jit(solution)/shard_map/ppermute | solution.py:19
  249.9 33.6 %collective-permute-start.14 = (f32[64,1024]{1,0:T(8,128)S(1)}, f32[64,1024]{1,0:T(8,128)S(1)}, u32[]{:S(2)}, u32[]{:S(2)}) collective-permute-start(f32[64,1024]{1,0:T(8,128)S(1)} %get-tuple-element.384), channel_id=1, source_target_pairs={{0,2},{1,3},{2,0},{3,1},{4,6},{5,7},{6,4},{7,5},{8,10},{9,11},{10,... | collective-permute-start | bytes 786440 | tf_op jit(solution)/shard_map/ppermute | solution.py:19
  286.4 32.4 %collective-permute-start.61 = (f32[256,512]{1,0:T(8,128)}, f32[256,512]{1,0:T(8,128)S(1)}, u32[]{:S(2)}, u32[]{:S(2)}) collective-permute-start(f32[256,512]{1,0:T(8,128)} %get-tuple-element.309), channel_id=1, source_target_pairs={{0,24},{4,28},{8,16},{12,20},{16,8},{20,12},{24,0},{28,4},{1,25},{... | collective-permute-start | bytes 1572872 | tf_op jit(solution)/shard_map/ppermute | solution.py:19
  290.4 16.7 %collective-permute-start.36 = (f32[520,128]{1,0:T(8,128)S(1)}, f32[520,128]{1,0:T(8,128)S(1)}, u32[]{:S(2)}, u32[]{:S(2)}) collective-permute-start(f32[520,128]{1,0:T(8,128)S(1)} %get-tuple-element.262.refs_1_), channel_id=1, source_target_pairs={{0,8},{4,12},{8,0},{12,4},{16,24},{20,28},{24,16},{28,20},{1,9},{5... | collective-permute-start | bytes 798728 | tf_op jit(solution)/shard_map/ppermute | solution.py:19
  290.5 25.6 %collective-permute-start.16 = (f32[64,1024]{1,0:T(8,128)S(1)}, f32[64,1024]{1,0:T(8,128)S(1)}, u32[]{:S(2)}, u32[]{:S(2)}) collective-permute-start(f32[64,1024]{1,0:T(8,128)S(1)} %get-tuple-element.211.refs_1_), channel_id=1, source_target_pairs={{0,1},{1,0},{2,3},{3,2},{4,5},{5,4},{6,7},{7,6},{8,9},{9,8},{10,11... | collective-permute-start | bytes 786440 | tf_op jit(solution)/shard_map/ppermute | solution.py:19
  292.0 24.2 %collective-permute-start.17 = (f32[64,1024]{1,0:T(8,128)S(1)}, f32[64,1024]{1,0:T(8,128)}, u32[]{:S(2)}, u32[]{:S(2)}) collective-permute-start(f32[64,1024]{1,0:T(8,128)S(1)} %collective-permute-done.15.refs_2_), channel_id=1, source_target_pairs={{0,1},{1,0},{2,3},{3,2},{4,5},{5,4},{6,7},{7,6},{8,9},{9,8},{10,11... | collective-permute-start | bytes 786440 | tf_op jit(solution)/shard_map/ppermute | solution.py:19
  307.2 18.1 %collective-permute-start.37 = (f32[520,128]{1,0:T(8,128)S(1)}, f32[520,128]{1,0:T(8,128)S(1)}, u32[]{:S(2)}, u32[]{:S(2)}) collective-permute-start(f32[520,128]{1,0:T(8,128)S(1)} %get-tuple-element.265), channel_id=1, source_target_pairs={{0,24},{4,28},{8,16},{12,20},{16,8},{20,12},{24,0},{28,4},{1,25},{... | collective-permute-start | bytes 798728 | tf_op jit(solution)/shard_map/ppermute | solution.py:19
  336.2 109.8 %collective-permute-start.68 = (f32[512,512]{1,0:T(8,128)}, f32[512,512]{1,0:T(8,128)}, u32[]{:S(2)}, u32[]{:S(2)}) collective-permute-start(f32[512,512]{1,0:T(8,128)} %get-tuple-element.325), channel_id=1, source_target_pairs={{0,24},{4,28},{8,16},{12,20},{16,8},{20,12},{24,0},{28,4},{1,25},{... | collective-permute-start | bytes 3145736 | tf_op jit(solution)/shard_map/ppermute | solution.py:19
  339.7 113.6 %collective-permute-start.54 = (f32[512,512]{1,0:T(8,128)}, f32[512,512]{1,0:T(8,128)S(1)}, u32[]{:S(2)}, u32[]{:S(2)}) collective-permute-start(f32[512,512]{1,0:T(8,128)} %get-tuple-element.295), channel_id=1, source_target_pairs={{0,4},{4,0},{8,12},{12,8},{16,20},{20,16},{24,28},{28,24},{1,5},{5... | collective-permute-start | bytes 3145736 | tf_op jit(solution)/shard_map/ppermute | solution.py:19
  346.9 107.4 %collective-permute-start.57 = (f32[512,512]{1,0:T(8,128)}, f32[512,512]{1,0:T(8,128)}, u32[]{:S(2)}, u32[]{:S(2)}) collective-permute-start(f32[512,512]{1,0:T(8,128)} %get-tuple-element.301), channel_id=1, source_target_pairs={{0,8},{4,12},{8,0},{12,4},{16,24},{20,28},{24,16},{28,20},{1,9},{5... | collective-permute-start | bytes 3145736 | tf_op jit(solution)/shard_map/ppermute | solution.py:19
  352.8 34.3 %collective-permute-start.49 = (f32[72,128]{1,0:T(8,128)S(1)}, f32[72,128]{1,0:T(8,128)S(1)}, u32[]{:S(2)}, u32[]{:S(2)}) collective-permute-start(f32[72,128]{1,0:T(8,128)S(1)} %pad_bitcast_fusion), channel_id=1, source_target_pairs={{0,8},{4,12},{8,0},{12,4},{16,24},{20,28},{24,16},{28,20},{1,9},{5... | collective-permute-start | bytes 110600 | tf_op jit(solution)/shard_map/ppermute | solution.py:19
  389.6 18.6 %collective-permute-start.63 = (f32[512,144]{1,0:T(8,128)}, f32[512,144]{1,0:T(8,128)}, u32[]{:S(2)}, u32[]{:S(2)}) collective-permute-start(f32[512,144]{1,0:T(8,128)} %pad_maximum_fusion.3), channel_id=1, source_target_pairs={{0,4},{4,0},{8,12},{12,8},{16,20},{20,16},{24,28},{28,24},{1,5},{5... | collective-permute-start | bytes 884744 | tf_op jit(solution)/shard_map/ppermute | solution.py:19
  454.3 16.0 %collective-permute-start.55 = (f32[256,512]{1,0:T(8,128)}, f32[256,512]{1,0:T(8,128)S(1)}, u32[]{:S(2)}, u32[]{:S(2)}) collective-permute-start(f32[256,512]{1,0:T(8,128)} %get-tuple-element.297), channel_id=1, source_target_pairs={{0,8},{4,12},{8,0},{12,4},{16,24},{20,28},{24,16},{28,20},{1,9},{5... | collective-permute-start | bytes 1572872 | tf_op jit(solution)/shard_map/ppermute | solution.py:19
  458.4 22.5 %collective-permute-start.58 = (f32[256,512]{1,0:T(8,128)}, f32[256,512]{1,0:T(8,128)S(1)}, u32[]{:S(2)}, u32[]{:S(2)}) collective-permute-start(f32[256,512]{1,0:T(8,128)} %get-tuple-element.303), channel_id=1, source_target_pairs={{0,24},{4,28},{8,16},{12,20},{16,8},{20,12},{24,0},{28,4},{1,25},{... | collective-permute-start | bytes 1572872 | tf_op jit(solution)/shard_map/ppermute | solution.py:19
  464.5 21.9 %collective-permute-start.70 = (f32[128,512]{1,0:T(8,128)}, f32[128,512]{1,0:T(8,128)}, u32[]{:S(2)}, u32[]{:S(2)}) collective-permute-start(f32[128,512]{1,0:T(8,128)} %get-tuple-element.329), channel_id=1, source_target_pairs={{0,8},{4,12},{8,0},{12,4},{16,24},{20,28},{24,16},{28,20},{1,9},{5... | collective-permute-start | bytes 786440 | tf_op jit(solution)/shard_map/ppermute | solution.py:19
  470.4 21.4 %collective-permute-start.56 = (f32[128,512]{1,0:T(8,128)S(1)}, f32[128,512]{1,0:T(8,128)S(1)}, u32[]{:S(2)}, u32[]{:S(2)}) collective-permute-start(f32[128,512]{1,0:T(8,128)S(1)} %get-tuple-element.299), channel_id=1, source_target_pairs={{0,24},{4,28},{8,16},{12,20},{16,8},{20,12},{24,0},{28,4},{1,25},{... | collective-permute-start | bytes 786440 | tf_op jit(solution)/shard_map/ppermute | solution.py:19
  (244 other events, 2337.6 us)
